TPU v7x, 256 devices: a whole 4x4x8 slice. The times are simulated.
256 devices in a mesh: dp: 8 (over z), ctx: 32 (over x, y, core).
Axes of the slice: x: 4, y: 4, z: 8, core: 2. Of those that a mesh axis runs over, the one named last changes fastest.
Arguments:
- head_inputs: bfloat16 [8, 4096, 2048], P('dp', 'ctx'), may hold values from -11 to 11
- entry_operator: bfloat16 [8, 4096, 128], P('dp', 'ctx'), may hold values from -3 to 3
- memory_readout: bfloat16 [8, 4096, 128], P('dp', 'ctx'), may hold values from -0.1796875 to 0.1796875
- unshifted_strides: float32 [8, 64, 4096], P('dp', None, 'ctx'), may hold values from -1.5 to 5.5, as said below
- log_decay_rates: float32 [64], P('dp'), may hold values from -11 to -2
- stride_shift: float32 [64], P('dp'), may hold values from -0.5 to 0.5
- bypass_coefficients: float32 [64], P('dp'), may hold values from 0.5 to 1.5
- result_cotangent: bfloat16 [8, 4096, 2048], P('dp', 'ctx'), may hold values from -26 to 26
Outputs:
- output: bfloat16 [8, 4096, 2048], P('dp', 'ctx')
- channels_grad: bfloat16 [8, 4096, 2048], P('dp', 'ctx')
- input_map_grad: float32 [8, 4096, 128], P('dp', 'ctx')
- output_map_grad: float32 [8, 4096, 128], P('dp', 'ctx')
- timestep_raw_gradient: float32 [8, 64, 4096], P('dp', None, 'ctx')
- a_log_grad: float32 [64], P('dp')
- bias_grad: float32 [64], P('dp')
- skip_grad: float32 [64], P('dp')
Inputs may be any that keep to these rules, and one draw needn't show every extreme that they name: `unshifted_strides`: step sizes are moderate at most positions, with a few large ones in each sequence.
All inputs are finite; a program needn't handle non-finite values.
Results may differ from a plain program's by a relative error of at most 0.001.
Values sent between devices are 32-bit elements; how exact they have to be, the bound alone decides.
A program may use at most 128 MiB of HBM per device.

v0:
```python
import jax
import jax.numpy as jnp
from jax import lax
from jax.sharding import Mesh
from jax.sharding import PartitionSpec as P

CTX = ("ctx_0", "ctx_1", "ctx_2")


maximal_accuracy = lax.Precision.HIGHEST


def rows_first(arrays, axis, dims):
    turned = [jnp.moveaxis(a, dim, 0) for a, dim in zip(arrays, dims)]
    widths = [t[0].size for t in turned]
    both = jnp.concatenate([t.reshape(-1, w) for t, w in zip(turned, widths)], axis=1)
    result = lax.all_gather(both, axis, axis=0, tiled=True)
    tiles = jnp.split(result, [sum(widths[:k]) for k in range(1, len(widths))], axis=1)
    return tuple(
        (
            jnp.moveaxis(b.reshape(-1, *t.shape[1:]), 0, dim)
            for b, t, dim in zip(tiles, turned, dims)
        )
    )


def nothing_yet(array, identity):
    return jax.tree.map(
        lambda a, e: jnp.broadcast_to(jnp.asarray(e, a.dtype), a.shape), array, identity
    )


def entering(array, axes, combine, identity, reverse):
    before = start = nothing_yet(array, identity)
    subtotal = array
    for axis in reversed(axes):
        devices, position = (lax.axis_size(axis), lax.axis_index(axis))
        pieces = jax.tree.map(lambda part: lax.all_gather(part, axis), subtotal)
        inside, subtotal = (start, start)
        for k in reversed(range(devices)) if reverse else range(devices):
            passed = k > position if reverse else k < position
            subtotal = combine(subtotal, jax.tree.map(lambda part: part[k], pieces))
            inside = jax.tree.map(lambda new, old: jnp.where(passed, new, old), subtotal, inside)
        before = combine(inside, before)
    return before


def split_up(array, dim, devices):
    dims = array.shape
    tiles = array.reshape(*dims[:dim], devices, dims[dim] // devices, *dims[dim + 1 :])
    return jnp.moveaxis(tiles, dim, 0)


def summed_on_arrival(array, axis, dim):
    devices = lax.axis_size(axis)
    tiles = lax.all_to_all(split_up(array, dim, devices), axis, 0, 0, tiled=True)
    return jnp.sum(tiles, axis=0)


def copy_for_each(array, axis):
    devices = lax.axis_size(axis)
    return lax.all_to_all(
        jnp.broadcast_to(array[None], (devices, *array.shape)), axis, 0, 0, tiled=True
    )


def of_everyone(array, axis):
    everything = copy_for_each(array, axis)
    return jnp.sum(everything, axis=0)


def packed_total(arrays, axis):
    vector, at, gathered = (jnp.concatenate([a.reshape(-1) for a in arrays]), 0, [])
    subtotal = of_everyone(vector, axis)
    for a in arrays:
        gathered.append(subtotal[at : at + a.size].reshape(a.shape))
        at += a.size
    return tuple(gathered)


def local_part(xg, write_operator, gram, dtr, rate_log, bias, skip):
    count = xg.shape[0]
    heads = dtr.shape[0]
    xg3 = xg.reshape(count, heads, -1)
    step = jax.nn.softplus(dtr + bias[:, None])
    logdecay = -jnp.exp(rate_log)[:, None] * step
    cum = jnp.cumsum(logdecay, axis=1)
    rows = lax.broadcasted_iota(jnp.int32, (count, count), 0)
    cols = lax.broadcasted_iota(jnp.int32, (count, count), 1)
    diff = cum[:, :, None] - cum[:, None, :]
    seg = jnp.exp(jnp.where((rows >= cols)[None], diff, -jnp.inf))
    weights = gram[None] * seg * step[:, None, :]
    inner = jnp.einsum("hts,shp->thp", weights, xg3, precision=maximal_accuracy)
    y_part = inner + skip[None, :, None] * xg3
    tail = jnp.exp(cum[:, -1:] - cum) * step
    scaled = xg3 * tail.T[:, :, None]
    state = jnp.einsum("shp,sn->hpn", scaled, write_operator, precision=maximal_accuracy)
    return (y_part, state, jnp.exp(cum))


def combine(earlier, later):
    return (earlier[0] * later[0], later[0][:, None, None] * earlier[1] + later[1])


def local(
    head_inputs,
    entry_operator,
    memory_readout,
    unshifted_strides,
    log_decay_rates,
    stride_shift,
    bypass_coefficients,
    result_cotangent,
):
    rate_all, full_bias_vector, skip_all = rows_first(
        (log_decay_rates, stride_shift, bypass_coefficients), "dp", (0, 0, 0)
    )
    tokens = head_inputs[0].astype(jnp.float32)
    write_operator = entry_operator[0].astype(jnp.float32)
    cmat = memory_readout[0].astype(jnp.float32)
    gram = lax.dot_general(
        memory_readout[0],
        entry_operator[0],
        (((1,), (1,)), ((), ())),
        preferred_element_type=jnp.float32,
    )
    raw = unshifted_strides[0]
    upstream = result_cotangent[0].astype(jnp.float32)
    heads = raw.shape[0]
    width = tokens.shape[1] // heads
    count = tokens.shape[0]
    parts = 1
    per = heads // parts
    output_pieces, dx_list, dt_list, rate_list, bias_list, skip_list = ([], [], [], [], [], [])
    cmat_grad = jnp.zeros_like(cmat)
    (y_part, state, growth_factor), backward = jax.vjp(
        local_part, tokens, write_operator, gram, raw, rate_all, full_bias_vector, skip_all
    )
    ends = growth_factor[:, -1]
    identity = (jnp.ones_like(ends), jnp.zeros_like(state))
    _, carried = entering((ends, state), CTX, combine, identity, False)
    readout = jnp.einsum("tn,hpn->thp", cmat, carried, precision=maximal_accuracy)
    output_pieces.append(y_part + growth_factor.T[:, :, None] * readout)
    g_group = upstream.reshape(count, per, width)
    dread = growth_factor.T[:, :, None] * g_group
    growth_grad = jnp.einsum("thp,thp->ht", g_group, readout, precision=maximal_accuracy)
    local_grad = jnp.einsum("thp,tn->hpn", dread, cmat, precision=maximal_accuracy)
    cmat_grad = cmat_grad + jnp.einsum("thp,hpn->tn", dread, carried, precision=maximal_accuracy)
    _, later = entering((ends, local_grad), CTX, combine, identity, True)
    end_grad = jnp.sum(later * carried, axis=(1, 2))
    growth_grad = growth_grad.at[:, -1].add(end_grad)
    grads = backward((g_group, later, growth_grad))
    dx_list.append(grads[0])
    bmat_grad = grads[1]
    gram_grad = grads[2]
    dt_list.append(grads[3])
    rate_list.append(grads[4])
    bias_list.append(grads[5])
    skip_list.append(grads[6])
    cmat_grad = cmat_grad + jnp.dot(gram_grad, write_operator, precision=maximal_accuracy)
    bmat_grad = bmat_grad + jnp.dot(gram_grad.T, cmat, precision=maximal_accuracy)
    core = output_pieces[0].reshape(count, heads * width)
    channels_grad = dx_list[0]
    timestep_raw_gradient = dt_list[0]
    rate_grad = rate_list[0]
    bias_grad = bias_list[0]
    skip_grad = skip_list[0]
    shares = (
        summed_on_arrival(rate_grad, "dp", 0),
        summed_on_arrival(bias_grad, "dp", 0),
        summed_on_arrival(skip_grad, "dp", 0),
    )
    owned = packed_total((shares[0], shares[1], shares[2]), CTX)
    return (
        core.astype(jnp.bfloat16)[None],
        channels_grad.astype(jnp.bfloat16)[None],
        bmat_grad[None],
        cmat_grad[None],
        timestep_raw_gradient[None],
        owned[0],
        owned[1],
        owned[2],
    )


def solution(mesh):
    torus = Mesh(mesh.devices.reshape(mesh.shape["dp"], 4, 4, 2), ("dp", "ctx_0", "ctx_1", "ctx_2"))
    return jax.shard_map(
        local,
        mesh=torus,
        in_specs=(
            P("dp", CTX, None),
            P("dp", CTX, None),
            P("dp", CTX, None),
            P("dp", None, CTX),
            P("dp"),
            P("dp"),
            P("dp"),
            P("dp", CTX, None),
        ),
        out_specs=(
            P("dp", CTX, None),
            P("dp", CTX, None),
            P("dp", CTX, None),
            P("dp", CTX, None),
            P("dp", None, CTX),
            P("dp"),
            P("dp"),
            P("dp"),
        ),
        check_vma=False,
    )
```

profile of v0, /device:TPU:1, one launch (start us, length us, event | category | flops | bytes accessed | tf_op | source)
XLA Modules:
  0.0 376.4 jit_solution(17329192003138858828)
XLA Ops:
  7.2 0.7 maximum_bitcast_fusion
  7.9 20.4 %all-gather.4 = f32[8,8,3]{1,2,0:T(4,128)S(1)} all-gather(f32[1,8,3]{1,2,0:T(4,128)S(1)} %maximum_bitcast_fusion), channel_id=1, replica_groups=mesh['dp'=8,'ctx_0'=4,'ctx_1'=4,'ctx_2'=2] {'dp'}, dimensions={0}, use_global_device_ids=true | all-gather | bytes 864 | tf_op jit(solution)/shard_map/all_gather | solution.py:17
  28.5 0.5 fusion.90
  29.0 0.8 broadcast_multiply_fusion
  29.8 0.3 reduce_window_sum.22
  30.1 0.2 slice_reduce_fusion
  30.3 0.9 exponential_bitcast_fusion
  31.2 1.3 copy.70
  32.5 1.5 copy.68
  34.1 0.4 fusion.44
  34.4 1.6 fusion.71
  36.2 1.6 fusion.75
  37.9 0.6 dynamic-slice.9
  38.5 0.6 dynamic-slice.8
  40.5 0.2 dynamic-update-slice.3
  40.8 8.6 %all-reduce.1 = f32[128]{0:T(128)S(1)} all-reduce(f32[128]{0:T(128)S(1)} %dynamic-update-slice.3), channel_id=2, replica_groups=mesh['dp'=8,'ctx_0'=4,'ctx_1'=4,'ctx_2'=2] {'ctx_2'}, use_global_device_ids=true, to_apply=%add.1 | all-reduce | flops 128 | bytes 1024
  49.5 7.6 %all-gather.24.cloned.1.call-done = f32[128,32,128]{2,1,0:T(8,128)} async-done(((f32[64,32,128]{2,1,0:T(8,128)}), f32[128,32,128]{2,1,0:T(8,128)}) %all-gather.24.cloned.1.call-update) | async-done | bytes 2097168 | tf_op jit(solution)/shard_map/all_gather | solution.py:38
  57.1 2.8 bitcast_add_fusion.16
  60.0 8.2 %all-reduce.2 = f32[256]{0:T(256)S(1)} all-reduce(f32[256]{0:T(256)S(1)} %get-tuple-element.107), channel_id=5, replica_groups=mesh['dp'=8,'ctx_0'=4,'ctx_1'=4,'ctx_2'=2] {'ctx_1'}, use_global_device_ids=true, to_apply=%add.2 | all-reduce | flops 256 | bytes 2048
  68.3 7.8 %all-gather.22.cloned.1.call-done = f32[128,32,128]{2,1,0:T(8,128)} async-done(((f32[64,32,128]{2,1,0:T(8,128)}), f32[128,32,128]{2,1,0:T(8,128)}) %all-gather.22.cloned.1.call-update) | async-done | bytes 2097168 | tf_op jit(solution)/shard_map/all_gather | solution.py:38
  76.1 2.7 bitcast_add_fusion.18
  78.9 50.5 %all-gather.18.cloned.1.call-done = f32[4,64,32,128]{3,2,1,0:T(8,128)} async-done(((f32[1,64,32,128]{3,2,1,0:T(8,128)}), f32[4,64,32,128]{3,2,1,0:T(8,128)}) %all-gather.18.cloned.1.call-update) | async-done | bytes 4194320 | tf_op jit(solution)/shard_map/all_gather | solution.py:38
  129.4 52.9 %all-gather.14.cloned.1.call-done = f32[4,64,32,128]{3,2,1,0:T(8,128)} async-done(((f32[1,64,32,128]{3,2,1,0:T(8,128)}), f32[4,64,32,128]{3,2,1,0:T(8,128)}) %all-gather.14.cloned.1.call-update) | async-done | bytes 4194320 | tf_op jit(solution)/shard_map/all_gather | solution.py:38
  182.3 4.8 %multiply_add_fusion = (f32[1,64,32,128]{3,2,1,0:T(8,128)}, f32[1,64,32,128]{3,2,1,0:T(8,128)}) fusion(f32[4,64,32,128]{3,2,1,0:T(8,128)} %all-gather.18.cloned.1.call-done, f32[64]{0:T(128)S(1)} %get-tuple-element.98, f32[64]{0:T(128)S(1)} %get-tuple-element.97, f32[64]{0:T(128)S(1)} %get-tuple-element.95, f32[64]{0:T(128)S(1)} %get-tuple-element.96, ...), kind=kLoop, calls=%fused_computation.86 | loop fusion | flops 3670016 | bytes 10487296 | tf_op jit(solution)/shard_map/add | solution.py:102
  187.1 0.5 all-gather.16.cloned.1.call-update
  187.8 0.7 all_to_all.23
  188.5 6.7 %all-to-all-start.2 = ((f32[8,1,8]{2,1,0:T(1,128)}), f32[8,1,8]{2,1,0:T(1,128)S(1)}, u32[]{:S(2)}, u32[]{:S(2)}) async-start(f32[8,1,8]{2,1,0:T(1,128)} %bitcast.81), calls=%async_computation.2 | async-start | bytes 8192 | tf_op jit(solution)/shard_map/all_to_all | solution.py:56
  195.3 7.6 %all-gather.6 = f32[4,1,64]{2,1,0:T(1,128)S(1)} all-gather(f32[1,1,64]{2,1,0:T(1,128)S(1)} %get-tuple-element.92), channel_id=1, replica_groups=mesh['dp'=8,'ctx_0'=4,'ctx_1'=4,'ctx_2'=2] {'ctx_0'}, dimensions={0}, use_global_device_ids=true | all-gather | bytes 1280 | tf_op jit(solution)/shard_map/all_gather | solution.py:38
  202.9 6.2 %all-gather.5 = f32[4,1,64]{2,1,0:T(1,128)S(1)} all-gather(f32[1,1,64]{2,1,0:T(1,128)S(1)} %get-tuple-element.93), channel_id=1, replica_groups=mesh['dp'=8,'ctx_0'=4,'ctx_1'=4,'ctx_2'=2] {'ctx_0'}, dimensions={0}, use_global_device_ids=true | all-gather | bytes 1280 | tf_op jit(solution)/shard_map/all_gather | solution.py:38
  209.1 0.6 iota_compare_fusion
  209.8 0.8 fusion.78
  210.7 0.6 reduce_sum.179
  211.3 27.1 %all-gather.20.cloned.1.call-done = f32[4,64,32,128]{3,2,1,0:T(8,128)} async-done(((f32[1,64,32,128]{3,2,1,0:T(8,128)}), f32[4,64,32,128]{3,2,1,0:T(8,128)}) %all-gather.20.cloned.1.call-update) | async-done | bytes 4194320 | tf_op jit(solution)/shard_map/all_gather | solution.py:38
  238.4 5.0 %add_add_fusion = f32[1,64,32,128]{3,2,1,0:T(8,128)S(1)} fusion(f32[1,64,32,128]{3,2,1,0:T(8,128)} %get-tuple-element.100, f32[4,64,32,128]{3,2,1,0:T(8,128)} %all-gather.20.cloned.1.call-done, f32[4,64,32,128]{3,2,1,0:T(8,128)} %all-gather.18.cloned.1.call-done, f32[128,32,128]{2,1,0:T(8,128)} %all-gather.24.cloned.1.call-done, ...), kind=kLoop, calls=%fused_computation.85 | loop fusion | flops 7602176 | bytes 11537162 | tf_op jit(solution)/shard_map/add | solution.py:102
  243.4 1.0 copy-done.6
  244.4 1.9 convolution_bitcast_fusion.2
  246.3 45.0 %all-gather.16.cloned.1.call-done = f32[4,64,32,128]{3,2,1,0:T(8,128)} async-done(((f32[1,64,32,128]{3,2,1,0:T(8,128)}), f32[4,64,32,128]{3,2,1,0:T(8,128)}) %all-gather.16.cloned.1.call-update) | async-done | bytes 4194320 | tf_op jit(solution)/shard_map/all_gather | solution.py:38
  291.3 8.6 %fusion.50 = f32[64]{0:T(128)S(1)} fusion(f32[4,64,32,128]{3,2,1,0:T(8,128)} %all-gather.20.cloned.1.call-done, f32[4,64,32,128]{3,2,1,0:T(8,128)} %all-gather.18.cloned.1.call-done, f32[128,32,128]{2,1,0:T(8,128)} %all-gather.24.cloned.1.call-done, f32[4,64,32,128]{3,2,1,0:T(8,128)} %all-gather.16.cloned.1.call-done, ...), kind=kLoop, calls=%fused_computation.49 | loop fusion | flops 16777152 | bytes 20977428 | tf_op jit(solution)/shard_map/reduce_sum | solution.py:150
  300.0 3.0 fusion.43
  303.0 1.3 fusion.95
  304.3 1.4 copy.73
  305.6 4.4 %add_add_fusion.1 = f32[1,64,32,128]{3,2,1,0:T(8,128)S(1)} fusion(f32[1,64,32,128]{3,2,1,0:T(8,128)} %get-tuple-element.101, f32[4,64,32,128]{3,2,1,0:T(8,128)} %all-gather.16.cloned.1.call-done, f32[4,64,32,128]{3,2,1,0:T(8,128)} %all-gather.14.cloned.1.call-done, f32[128,32,128]{2,1,0:T(8,128)S(1)} %copy-done.1, f32[64]{0:T(128)S(1)} %get-tuple-element.71, ...), kind=kLoop, calls=%fused_computation.89 | loop fusion | flops 7602176 | bytes 11537162 | tf_op jit(solution)/shard_map/add | solution.py:102
  310.0 1.0 copy-done.4
  311.0 1.7 fusion.59
  312.8 0.2 scatter-add.4
  313.0 4.9 %fusion.7 = (f32[64,128]{1,0:T(8,128)S(1)}, f32[64,128]{1,0:T(8,128)S(1)}, f32[64,128]{1,0:T(8,128)S(1)}, f32[128,128]{1,0:T(8,128)S(1)}) fusion(f32[64,128]{1,0:T(8,128)} %get-tuple-element.76, f32[64,128]{1,0:T(8,128)S(1)} %reduce_window_sum.22, f32[128,128]{1,0:T(8,128)} %fusion.78, pred[128,128]{1,0:T(8,128)(4,1)} %iota_compare_fusion, ...), kind=kOutput, calls=%fused_computation.9 | convolution fusion | flops 80699392 | bytes 1359872 | tf_op jit(solution)/shard_map/transpose(jvp(hts,shp->thp))/dot_general | solution.py:93
  318.0 1.2 reduce_window_sum.23
  319.2 0.8 fusion.93
  320.1 0.7 all_to_all.21
  320.8 6.7 %all-to-all-start.1 = ((f32[8,1,8]{2,1,0:T(1,128)}), f32[8,1,8]{2,1,0:T(1,128)S(1)}, u32[]{:S(2)}, u32[]{:S(2)}) async-start(f32[8,1,8]{2,1,0:T(1,128)} %bitcast.80), calls=%async_computation.1 | async-start | bytes 8192 | tf_op jit(solution)/shard_map/all_to_all | solution.py:56
  327.6 5.7 %fusion.38 = bf16[128,64,32]{0,2,1:T(8,128)(2,1)S(1)} fusion(bf16[128,64,32]{0,2,1:T(8,128)(2,1)S(1)} %bitcast.326, f32[64,128]{1,0:T(8,128)} %get-tuple-element.76, f32[64,128]{1,0:T(8,128)S(1)} %reduce_window_sum.22, f32[128,128]{1,0:T(8,128)} %fusion.78, pred[128,128]{1,0:T(8,128)(4,1)} %iota_compare_fusion, f32[64,32,128]{2,1,0:T(8,128)} %get-tuple-element.113, ...), kind=kOutput, calls=%fused_computation.34 | convolution fusion | flops 408420352 | bytes 2277632 | tf_op jit(solution)/shard_map/jvp(hts,shp->thp)/dot_general | solution.py:93
  333.4 3.5 fusion.35
  337.0 1.8 convolution_bitcast_fusion.1
  338.9 0.6 mul.728
  339.5 6.6 %all-to-all-start = ((f32[8,1,8]{2,1,0:T(1,128)}), f32[8,1,8]{2,1,0:T(1,128)S(1)}, u32[]{:S(2)}, u32[]{:S(2)}) async-start(f32[8,1,8]{2,1,0:T(1,128)} %bitcast.79), calls=%async_computation | async-start | bytes 8192 | tf_op jit(solution)/shard_map/all_to_all | solution.py:56
  346.1 0.8 fusion.41
  347.0 5.6 %all-to-all-done = f32[8,1,8]{2,1,0:T(1,128)S(1)} async-done(((f32[8,1,8]{2,1,0:T(1,128)}), f32[8,1,8]{2,1,0:T(1,128)S(1)}, u32[]{:S(2)}, u32[]{:S(2)}) %all-to-all-start) | async-done | bytes 288 | tf_op jit(solution)/shard_map/all_to_all | solution.py:56
  352.7 0.6 broadcast_in_dim.71
  353.3 8.6 %all-to-all-start.3 = ((f32[32,1,24]{2,1,0:T(1,128)}), f32[32,1,24]{2,1,0:T(1,128)S(1)}, u32[]{:S(2)}, u32[]{:S(2)}) async-start(f32[32,1,24]{2,1,0:T(1,128)} %broadcast_in_dim.71), calls=%async_computation.3 | async-start | bytes 32768 | tf_op jit(solution)/shard_map/all_to_all | solution.py:62
  361.9 0.9 fusion.42
  362.8 1.0 copy.78
  363.8 1.0 copy.79
  364.8 4.0 %all-to-all-done.3 = f32[32,1,24]{2,1,0:T(1,128)S(1)} async-done(((f32[32,1,24]{2,1,0:T(1,128)}), f32[32,1,24]{2,1,0:T(1,128)S(1)}, u32[]{:S(2)}, u32[]{:S(2)}) %all-to-all-start.3) | async-done | bytes 3104 | tf_op jit(solution)/shard_map/all_to_all | solution.py:62
  368.9 0.6 fusion.97
  (86 shorter events, 1.9 us)
Async XLA Ops:
  7.2 29.0 %copy-start = (bf16[1,128,128]{2,1,0:T(8,128)(2,1)S(1)}, bf16[1,128,128]{2,1,0:T(8,128)(2,1)}, u32[]{:S(2)}) copy-start(bf16[1,128,128]{2,1,0:T(8,128)(2,1)} %param.11) | copy-start | bytes 98308
  7.2 27.3 %copy-start.13 = (bf16[1,128,128]{2,1,0:T(8,128)(2,1)S(1)}, bf16[1,128,128]{2,1,0:T(8,128)(2,1)}, u32[]{:S(2)}) copy-start(bf16[1,128,128]{2,1,0:T(8,128)(2,1)} %param.12) | copy-start | bytes 98308
  7.2 49.9 %all-gather.24.cloned.1.call-start = ((), (), s32[]{:S(2)}) async-start(), calls=%async_computation.9 | async-start | bytes 3145728 | tf_op jit(solution)/shard_map/all_gather | solution.py:38
  32.5 5.3 %copy-start.7 = (bf16[1,128,2048]{1,2,0:T(8,128)(2,1)}, bf16[1,128,2048]{1,2,0:T(8,128)(2,1)S(1)}, u32[]{:S(2)}) copy-start(bf16[1,128,2048]{1,2,0:T(8,128)(2,1)S(1)} %copy.70) | copy-start | bytes 1572868
  34.0 3.8 copy-start.10
  34.0 3.8 %copy-start.25 = (u32[256]{0:T(256)S(1)}, u32[256]{0:T(256)}, u32[]{:S(2)}) copy-start(u32[256]{0:T(256)} %constant.82) | copy-start | bytes 3076
  34.1 4.4 %copy-start.24 = (u32[256]{0:T(256)S(1)}, u32[256]{0:T(256)}, u32[]{:S(2)}) copy-start(u32[256]{0:T(256)} %constant.77) | copy-start | bytes 3076
  34.4 25.5 %copy-start.2 = (f32[1,128,2048]{1,2,0:T(8,128)}, f32[1,128,2048]{1,2,0:T(8,128)S(1)}, u32[]{:S(2)}) copy-start(f32[1,128,2048]{1,2,0:T(8,128)S(1)} %get-tuple-element.74) | copy-start | bytes 3145732
  36.1 40.0 %all-gather.22.cloned.1.call-start = ((), (), s32[]{:S(2)}) async-start(), calls=%async_computation.8 | async-start | bytes 3145728 | tf_op jit(solution)/shard_map/all_gather | solution.py:38
  37.8 91.6 %all-gather.18.cloned.1.call-start = ((), (), s32[]{:S(2)}) async-start(), calls=%async_computation.6 | async-start | bytes 5242880 | tf_op jit(solution)/shard_map/all_gather | solution.py:38
  59.9 122.4 %all-gather.14.cloned.1.call-start = ((), (), s32[]{:S(2)}) async-start(), calls=%async_computation.4 | async-start | bytes 5242880 | tf_op jit(solution)/shard_map/all_gather | solution.py:38
  78.9 159.5 %all-gather.20.cloned.1.call-start = ((), (), s32[]{:S(2)}) async-start(), calls=%async_computation.7 | async-start | bytes 5242880 | tf_op jit(solution)/shard_map/all_gather | solution.py:38
  187.1 104.2 %all-gather.16.cloned.1.call-start = ((), (), s32[]{:S(2)}) async-start(), calls=%async_computation.5 | async-start | bytes 5242880 | tf_op jit(solution)/shard_map/all_gather | solution.py:38
  188.5 22.1 %all-to-all-start.2 = ((f32[8,1,8]{2,1,0:T(1,128)}), f32[8,1,8]{2,1,0:T(1,128)S(1)}, u32[]{:S(2)}, u32[]{:S(2)}) async-start(f32[8,1,8]{2,1,0:T(1,128)} %bitcast.81), calls=%async_computation.2 | async-start | bytes 8192 | tf_op jit(solution)/shard_map/all_to_all | solution.py:56
  209.7 81.6 %copy-start.19 = (f32[64]{0:T(128)}, f32[64]{0:T(128)S(1)}, u32[]{:S(2)}) copy-start(f32[64]{0:T(128)S(1)} %get-tuple-element.89) | copy-start | bytes 772
  209.7 81.6 %copy-start.20 = (f32[64]{0:T(128)}, f32[64]{0:T(128)S(1)}, u32[]{:S(2)}) copy-start(f32[64]{0:T(128)S(1)} %get-tuple-element.90) | copy-start | bytes 772
  209.7 81.6 %copy-start.21 = (f32[64]{0:T(128)}, f32[64]{0:T(128)S(1)}, u32[]{:S(2)}) copy-start(f32[64]{0:T(128)S(1)} %get-tuple-element.91) | copy-start | bytes 772
  238.4 6.0 %copy-start.3 = (f32[1,128,2048]{1,2,0:T(8,128)S(1)}, f32[1,128,2048]{1,2,0:T(8,128)}, u32[]{:S(2)}) copy-start(f32[1,128,2048]{1,2,0:T(8,128)} %copy-done.2) | copy-start | bytes 3145732
  238.4 52.9 %copy-start.1 = (f32[128,32,128]{2,1,0:T(8,128)S(1)}, f32[128,32,128]{2,1,0:T(8,128)}, u32[]{:S(2)}) copy-start(f32[128,32,128]{2,1,0:T(8,128)} %all-gather.22.cloned.1.call-done) | copy-start | bytes 6291460
  243.4 1.0 copy-start.6
  291.3 11.7 %copy-start.14 = (f32[1,64,128]{2,1,0:T(8,128)S(1)}, f32[1,64,128]{2,1,0:T(8,128)}, u32[]{:S(2)}) copy-start(f32[1,64,128]{2,1,0:T(8,128)} %param.13) | copy-start | bytes 98308
  305.6 5.4 %copy-start.8 = (bf16[1,128,2048]{1,2,0:T(8,128)(2,1)S(1)}, bf16[1,128,2048]{1,2,0:T(8,128)(2,1)}, u32[]{:S(2)}) copy-start(bf16[1,128,2048]{1,2,0:T(8,128)(2,1)} %copy-done.7) | copy-start | bytes 1572868
  310.0 1.0 copy-start.4
  313.0 4.9 %copy-start.15 = (f32[64,1]{1,0:T(8,128)S(1)}, f32[64,1]{1,0:T(8,128)}, u32[]{:S(2)}) copy-start(f32[64,1]{1,0:T(8,128)} %copy.73) | copy-start | bytes 772
  313.0 14.5 %copy-start.11 = (bf16[1,128,2048]{1,2,0:T(8,128)(2,1)S(1)}, bf16[1,128,2048]{1,2,0:T(8,128)(2,1)}, u32[]{:S(2)}) copy-start(bf16[1,128,2048]{1,2,0:T(8,128)(2,1)} %copy-done.10) | copy-start | bytes 1572868
  320.8 18.7 %all-to-all-start.1 = ((f32[8,1,8]{2,1,0:T(1,128)}), f32[8,1,8]{2,1,0:T(1,128)S(1)}, u32[]{:S(2)}, u32[]{:S(2)}) async-start(f32[8,1,8]{2,1,0:T(1,128)} %bitcast.80), calls=%async_computation.1 | async-start | bytes 8192 | tf_op jit(solution)/shard_map/all_to_all | solution.py:56
  327.5 5.8 %copy-start.9 = (bf16[1,128,2048]{1,2,0:T(8,128)(2,1)S(1)}, bf16[1,128,2048]{1,2,0:T(8,128)(2,1)}, u32[]{:S(2)}) copy-start(bf16[1,128,2048]{1,2,0:T(8,128)(2,1)} %copy-done.7) | copy-start | bytes 1572868
  327.5 5.8 %copy-start.12 = (f32[128,64,32]{0,2,1:T(8,128)S(1)}, f32[128,64,32]{0,2,1:T(8,128)}, u32[]{:S(2)}) copy-start(f32[128,64,32]{0,2,1:T(8,128)} %get-tuple-element.111) | copy-start | bytes 3145732
  327.5 5.8 %copy-start.16 = (f32[128,128]{1,0:T(8,128)S(1)}, f32[128,128]{1,0:T(8,128)}, u32[]{:S(2)}) copy-start(f32[128,128]{1,0:T(8,128)} %fusion.78) | copy-start | bytes 196612
  327.6 5.8 %copy-start.17 = (f32[64,128]{1,0:T(8,128)S(1)}, f32[64,128]{1,0:T(8,128)}, u32[]{:S(2)}) copy-start(f32[64,128]{1,0:T(8,128)} %get-tuple-element.76) | copy-start | bytes 98308
  327.6 5.8 %copy-start.18 = (pred[128,128]{1,0:T(8,128)(4,1)S(1)}, pred[128,128]{1,0:T(8,128)(4,1)}, u32[]{:S(2)}) copy-start(pred[128,128]{1,0:T(8,128)(4,1)} %iota_compare_fusion) | copy-start | bytes 49156
  327.6 5.8 %copy-start.23 = (f32[64]{0:T(128)S(1)}, f32[64]{0:T(128)}, u32[]{:S(2)}) copy-start(f32[64]{0:T(128)} %get-tuple-element.81) | copy-start | bytes 772
  333.4 3.6 copy-start.5
  333.4 19.2 %copy-start.22 = (f32[8]{0:T(128)S(1)}, f32[8]{0:T(128)}, u32[]{:S(2)}) copy-start(f32[8]{0:T(128)} %reduce_sum.179) | copy-start | bytes 100
  339.5 13.1 %all-to-all-start = ((f32[8,1,8]{2,1,0:T(1,128)}), f32[8,1,8]{2,1,0:T(1,128)S(1)}, u32[]{:S(2)}, u32[]{:S(2)}) async-start(f32[8,1,8]{2,1,0:T(1,128)} %bitcast.79), calls=%async_computation | async-start | bytes 8192 | tf_op jit(solution)/shard_map/all_to_all | solution.py:56
  353.3 15.6 %all-to-all-start.3 = ((f32[32,1,24]{2,1,0:T(1,128)}), f32[32,1,24]{2,1,0:T(1,128)S(1)}, u32[]{:S(2)}, u32[]{:S(2)}) async-start(f32[32,1,24]{2,1,0:T(1,128)} %broadcast_in_dim.71), calls=%async_computation.3 | async-start | bytes 32768 | tf_op jit(solution)/shard_map/all_to_all | solution.py:62
Sparse Core Ops, SparseCore 0:
  36.2 20.8 all-gather.23
  58.9 17.1 all-gather.21
  77.9 51.4 all-gather.17
  131.1 51.1 all-gather.13
  187.2 51.1 all-gather.19
  240.1 51.1 all-gather.15
where the time goes:
time: 377 us; the launch traced here: 376 us
  waiting for transfers between devices  201 us (53%)
  blocking collectives  50.9 us (14%)
  other arithmetic  37.9 us (10%)
  starting transfers between devices  29 us (8%)
  matrix products  28.2 us (7%)
  between operations  15.9 us (4%)
  local copies, waits for them, and re-layouts  13.2 us (4%)
    all_gather x6, waiting for transfers between devices, entering(): pieces = jax.tree.map(lambda part: lax.all_gather(part, axis), subtotal)  191 us
    all_gather x1, blocking collectives, rows_first(): result = lax.all_gather(both, axis, axis=0, tiled=True)  20.4 us
    all_to_all x3, starting transfers between devices, summed_on_arrival(): lax.all_to_all(split_up(array, dim, devices), axis, 0, 0, tiled=True)  20.1 us
    add x5, other arithmetic, combine(): later[0][:, None, None] * earlier[1] + later[1]  19.6 us
    unnamed x2, blocking collectives  16.7 us
    dot_general x3, matrix products, local_part(): inner = jnp.einsum('hts,shp->thp', weights, xg3, precision=maximal_accuracy)  14.2 us
    all_gather x2, blocking collectives, entering(): pieces = jax.tree.map(lambda part: lax.all_gather(part, axis), subtotal)  13.7 us
    all_to_all x1, starting transfers between devices, copy_for_each(): lax.all_to_all(jnp.broadcast_to(array[None], (devices, *array.shape)), ax...  8.61 us
  transfers between devices with their start and end apart: 10, of which 8 were waited for; matrix products, arithmetic and copies ran while one was open for 9% of the time, Pallas kernels for 0%

commit v1 on v0

v1 whole, which is shorter than its diff:
```python
import functools

import jax
import jax.numpy as jnp
from jax import lax
from jax.experimental import pallas as pl
from jax.experimental.pallas import tpu as pltpu
from jax.sharding import PartitionSpec as P

MESH = pl.DeviceIdType.MESH
F32, BF16 = jnp.float32, jnp.bfloat16

TOKENS = 128
HEADS = 64
WIDTH = 32
ENTRIES = 128
ROWS = HEADS * WIDTH
HALF = ROWS // 2
GROUP = 8
GROUP_ROWS = GROUP * WIDTH
GROUPS = HEADS // GROUP
CHIPS = 16
PIECE = HALF // CHIPS
SPLIT = (4, 6)


def split(value):
    high = value.astype(BF16)
    return high, (value - high.astype(F32)).astype(BF16)


def mul(a, b):
    return jnp.dot(a, b, preferred_element_type=F32)


def mul_nt(a, b):
    return lax.dot_general(a, b, (((1,), (1,)), ((), ())), preferred_element_type=F32)


def spread(rows, width=WIDTH):
    count = rows.shape[0]
    parts = [jnp.broadcast_to(rows[k : k + 1, :], (width, rows.shape[1])) for k in range(count)]
    return jnp.concatenate(parts, axis=0)


def folded(value, count):
    return jnp.sum(value.reshape(count, WIDTH, value.shape[1]), axis=1)


def lane_sums(value, reverse):
    lanes = lax.broadcasted_iota(jnp.int32, value.shape, 1)
    size = value.shape[1]
    shift = 1
    while shift < size:
        if reverse:
            moved = jnp.where(lanes < size - shift, pltpu.roll(value, size - shift, 1), 0.0)
        else:
            moved = jnp.where(lanes >= shift, pltpu.roll(value, shift, 1), 0.0)
        value = value + moved
        shift *= 2
    return value


def kernel(
    x_ref, b_ref, c_ref, raw_ref, rate_ref, bias_ref, skip_ref, g_ref,
    y_out, dx_out, db_out, dc_out, dt_out, rate_out, bias_out, skip_out,
    xt, gt, gram_t, par_recv, cum_s, step_s, tail_s, grow_s, skip_s, cum_col, step_col,
    tx_hi, tx_lo, eg_hi, eg_lo, txn_hi, txn_lo, egn_hi, egn_lo,
    ends_own, ends_other, state, grad, state_other, grad_other,
    tot_f, tot_b, got_f, got_b, pre_f, pre_b, in_f, in_b, back_f, back_b, carried, later,
    y_t, d_t, dgram_t, u_s, v_s, sk_s, share, share_got, total, total_got,
    par_ss, par_rs, pair_ss, pair_rs, f1_ss, f1_rs, b1_ss, b1_rs, f2_ss, f2_rs, b2_ss, b2_rs,
    back_ss, back_rs, share_ss, share_rs, total_ss, total_rs,
):
    me = lax.axis_index("ctx")
    dp = lax.axis_index("dp")
    n_dp = lax.axis_size("dp")
    n_ctx = lax.axis_size("ctx")
    core = lax.rem(me, 2)
    chip = me // 2
    partner = chip * 2 + 1 - core
    first = core == 0

    def to(src, dst, ss, rs, where):
        return pltpu.make_async_remote_copy(src, dst, ss, rs, device_id=where, device_id_type=MESH)

    barrier = pltpu.get_barrier_semaphore()
    for k in range(1, n_dp):
        pl.semaphore_signal(barrier, 1, device_id={"dp": lax.rem(dp + k, n_dp)}, device_id_type=MESH)
    for k in range(1, n_ctx):
        pl.semaphore_signal(barrier, 1, device_id={"ctx": lax.rem(me + k, n_ctx)}, device_id_type=MESH)

    lanes8 = lax.broadcasted_iota(jnp.int32, (8, 128), 1)
    rows8 = lax.broadcasted_iota(jnp.int32, (8, 128), 0)
    tile = jnp.zeros((8, 128), F32)
    for row, ref in enumerate((rate_ref, bias_ref, skip_ref)):
        for j in range(8):
            here = jnp.logical_and(rows8 == row, lanes8 == dp * 8 + j)
            tile = jnp.where(here, ref[j], tile)
    par_recv[dp] = tile

    for k in range(GROUPS):
        at = slice(k * GROUP_ROWS, (k + 1) * GROUP_ROWS)
        xt[at, :] = jnp.transpose(x_ref[:, at].astype(F32)).astype(BF16)
        gt[at, :] = jnp.transpose(g_ref[:, at].astype(F32)).astype(BF16)
    gram_t[...] = mul_nt(b_ref[...], c_ref[...])

    pl.semaphore_wait(barrier, n_dp + n_ctx - 2)

    sends = []
    for k in range(1, n_dp):
        copy = to(par_recv.at[dp], par_recv.at[dp], par_ss.at[k], par_rs.at[k], {"dp": lax.rem(dp + k, n_dp)})
        copy.start()
        sends.append(copy)
    for copy in sends:
        copy.wait()

    params = par_recv[0]
    for k in range(1, n_dp):
        params = params + par_recv[k]
    columns = jnp.transpose(jnp.concatenate([params] * 16, axis=0))[:HEADS, :]
    square = (HEADS, 128)
    rate = jnp.broadcast_to(columns[:, 0:1], square)
    bias = jnp.broadcast_to(columns[:, 1:2], square)
    skip_s[...] = jnp.broadcast_to(columns[:, 2:3], square)
    z = raw_ref[...] + bias
    step = jnp.maximum(z, 0.0) + jnp.log1p(jnp.exp(-jnp.abs(z)))
    cum = lane_sums(-jnp.exp(rate) * step, False)
    last = jnp.broadcast_to(cum[:, 127:128], square)
    cum_s[...] = cum
    step_s[...] = step
    tail_s[...] = jnp.exp(last - cum) * step
    grow_s[...] = jnp.exp(cum)
    ends_own[...] = jnp.exp(last)

    def states(g):
        rows = pl.ds(pl.multiple_of(g * GROUP_ROWS, GROUP_ROWS), GROUP_ROWS)
        heads = pl.ds(pl.multiple_of(g * GROUP, GROUP), GROUP)
        hi, lo = split(xt[rows, :].astype(F32) * spread(tail_s[heads, :]))
        tx_hi[rows, :] = hi
        tx_lo[rows, :] = lo
        state[rows, :] = mul(hi, b_ref[...]) + mul(lo, b_ref[...])

    def grads(g):
        rows = pl.ds(pl.multiple_of(g * GROUP_ROWS, GROUP_ROWS), GROUP_ROWS)
        heads = pl.ds(pl.multiple_of(g * GROUP, GROUP), GROUP)
        hi, lo = split(gt[rows, :].astype(F32) * spread(grow_s[heads, :]))
        eg_hi[rows, :] = hi
        eg_lo[rows, :] = lo
        grad[rows, :] = mul(hi, c_ref[...]) + mul(lo, c_ref[...])

    mine = pl.ds(pl.multiple_of(core * HALF, HALF), HALF)
    theirs = pl.ds(pl.multiple_of((1 - core) * HALF, HALF), HALF)
    there = {"ctx": partner}
    half_groups = GROUPS // 2
    for k in range(half_groups):
        states((1 - core) * half_groups + k)
    pair = [
        to(ends_own, ends_other, pair_ss.at[0], pair_rs.at[0], there),
        to(state.at[theirs], state_other, pair_ss.at[1], pair_rs.at[1], there),
        to(grad.at[theirs], grad_other, pair_ss.at[2], pair_rs.at[2], there),
    ]
    pair[0].start()
    pair[1].start()
    for k in range(half_groups):
        grads((1 - core) * half_groups + k)
    pair[2].start()
    for k in range(half_groups):
        states(core * half_groups + k)
    for k in range(half_groups):
        grads(core * half_groups + k)

    base = core * (HEADS // 2)

    def row_of(ref, head):
        return jnp.broadcast_to(ref[pl.ds(head, 1), :], (WIDTH, 128))

    def two(ref, r):
        return jnp.concatenate([row_of(ref, base + 2 * r), row_of(ref, base + 2 * r + 1)], axis=0)

    pair[0].wait()
    pair[1].wait()
    for r in range(CHIPS):
        rows = pl.ds(pl.multiple_of(core * HALF + r * PIECE, PIECE), PIECE)
        e_own, e_other = two(ends_own, r), two(ends_other, r)
        own, other = state[rows, :], state_other[r * PIECE : (r + 1) * PIECE, :]
        tot_f[r, 0:PIECE, :] = jnp.where(first, e_other * own + other, own + e_own * other)
        decay = jnp.concatenate(
            [ends_own[pl.ds(base + 2 * r + k, 1), :] * ends_other[pl.ds(base + 2 * r + k, 1), :] for k in range(2)] * 4, axis=0
        )
        tot_f[r, PIECE : PIECE + 8, :] = decay
    got_f[chip] = tot_f[chip]

    def chip_of(k):
        return lax.rem(chip + k, CHIPS)

    def chip_id(k):
        return {"ctx": chip_of(k) * 2 + core}

    f1 = [to(tot_f.at[chip_of(k)], got_f.at[chip], f1_ss.at[k], f1_rs.at[k], chip_id(k)) for k in range(1, CHIPS)]
    for copy in f1:
        copy.start()

    pair[2].wait()
    for r in range(CHIPS):
        rows = pl.ds(pl.multiple_of(core * HALF + r * PIECE, PIECE), PIECE)
        e_own, e_other = two(ends_own, r), two(ends_other, r)
        own, other = grad[rows, :], grad_other[r * PIECE : (r + 1) * PIECE, :]
        tot_b[r] = jnp.where(first, own + e_own * other, e_other * own + other)
    got_b[chip] = tot_b[chip]
    b1 = [to(tot_b.at[chip_of(k)], got_b.at[chip], b1_ss.at[k], b1_rs.at[k], chip_id(k)) for k in range(1, CHIPS)]
    for copy in b1:
        copy.start()

    def padded(value):
        return jnp.transpose(jnp.concatenate([value, value], axis=0))

    cum_t, step_t = padded(cum_s[...]), padded(step_s[...])
    for k in range(GROUPS):
        cum_col[k] = cum_t[:, k * GROUP : (k + 1) * GROUP]
        step_col[k] = step_t[:, k * GROUP : (k + 1) * GROUP]
    dgram_t[...] = jnp.zeros_like(dgram_t)

    def within(g, _):
        rows = pl.ds(pl.multiple_of(g * GROUP_ROWS, GROUP_ROWS), GROUP_ROWS)
        heads = pl.ds(pl.multiple_of(g * GROUP, GROUP), GROUP)
        cum8, cumc, stepc = cum_s[heads, :], cum_col[g], step_col[g]
        xt8, gt8 = xt[rows, :], gt[rows, :]
        above = lax.broadcasted_iota(jnp.int32, (TOKENS, TOKENS), 0) <= lax.broadcasted_iota(
            jnp.int32, (TOKENS, TOKENS), 1
        )
        gram = gram_t[...]
        acc = dgram_t[...]
        none = jnp.zeros((WIDTH, TOKENS), BF16)
        for quad in range(2):
            xq = x_ref[:, pl.ds(pl.multiple_of(g * GROUP_ROWS + quad * 128, 128), 128)]
            for j in range(4):
                k = quad * 4 + j
                at = slice(k * WIDTH, (k + 1) * WIDTH)
                g_rows = gt8[at, :]
                weights_g = jnp.concatenate([g_rows if i == j else none for i in range(4)], axis=0)
                dw = mul(xq, weights_g)
                diff = jnp.broadcast_to(cum8[k : k + 1, :], (TOKENS, TOKENS)) - jnp.broadcast_to(
                    cumc[:, k : k + 1], (TOKENS, TOKENS)
                )
                seg = jnp.exp(jnp.where(above, diff, -1e30))
                factor = seg * jnp.broadcast_to(stepc[:, k : k + 1], (TOKENS, TOKENS))
                acc = acc + dw * factor
                hi, lo = split(gram * factor)
                inner = mul(xt8[at, :], hi) + mul(xt8[at, :], lo)
                back = mul_nt(g_rows, hi) + mul_nt(g_rows, lo)
                out = pl.ds(pl.multiple_of(g * GROUP_ROWS + k * WIDTH, WIDTH), WIDTH)
                y_t[out, :] = inner
                d_t[out, :] = back
        dgram_t[...] = acc
        sk_s[heads, :] = folded(xt8.astype(F32) * gt8.astype(F32), GROUP)
        return 0

    lax.fori_loop(0, SPLIT[0], within, 0)

    for copy in f1:
        copy.wait()
    run = jnp.zeros((PIECE, 128), F32)
    for q in range(CHIPS):
        pre_f[q] = run
        decay = jnp.concatenate(
            [jnp.broadcast_to(got_f[q, PIECE + k : PIECE + k + 1, :], (WIDTH, 128)) for k in range(2)], axis=0
        )
        run = decay * run + got_f[q, 0:PIECE, :]
    in_f[pl.ds(pl.multiple_of(chip * PIECE, PIECE), PIECE), :] = pre_f[chip]
    spot = pl.ds(pl.multiple_of(chip * PIECE, PIECE), PIECE)
    f2 = [to(pre_f.at[chip_of(k)], in_f.at[spot], f2_ss.at[k], f2_rs.at[k], chip_id(k)) for k in range(1, CHIPS)]
    for copy in f2:
        copy.start()

    lax.fori_loop(SPLIT[0], SPLIT[1], within, 0)

    for copy in b1:
        copy.wait()
    run = jnp.zeros((PIECE, 128), F32)
    for q in reversed(range(CHIPS)):
        pre_b[q] = run
        decay = jnp.concatenate(
            [jnp.broadcast_to(got_f[q, PIECE + k : PIECE + k + 1, :], (WIDTH, 128)) for k in range(2)], axis=0
        )
        run = decay * run + got_b[q]
    in_b[pl.ds(pl.multiple_of(chip * PIECE, PIECE), PIECE), :] = pre_b[chip]
    b2 = [to(pre_b.at[chip_of(k)], in_b.at[spot], b2_ss.at[k], b2_rs.at[k], chip_id(k)) for k in range(1, CHIPS)]
    for copy in b2:
        copy.start()

    lax.fori_loop(SPLIT[1], GROUPS, within, 0)

    def turn(k, _):
        rows = pl.ds(pl.multiple_of(k * 128, 128), 128)
        for src, dst in ((tx_hi, txn_hi), (tx_lo, txn_lo), (eg_hi, egn_hi), (eg_lo, egn_lo)):
            dst[:, rows] = jnp.transpose(src[rows, :].astype(F32)).astype(BF16)
        return 0

    lax.fori_loop(0, ROWS // 128, turn, 0)

    for copy in f2:
        copy.wait()
    for r in range(CHIPS):
        at = slice(r * PIECE, (r + 1) * PIECE)
        rows = pl.ds(pl.multiple_of(core * HALF + r * PIECE, PIECE), PIECE)
        e_own, e_other = two(ends_own, r), two(ends_other, r)
        chips = in_f[at, :]
        carried[rows, :] = jnp.where(first, chips, e_other * chips + state_other[at, :])
        back_f[at, :] = jnp.where(first, e_own * chips + state[rows, :], chips)
    back = [
        to(back_f, carried.at[mine], back_ss.at[0], back_rs.at[0], there),
        to(back_b, later.at[mine], back_ss.at[1], back_rs.at[1], there),
    ]
    back[0].start()
    for copy in b2:
        copy.wait()
    for r in range(CHIPS):
        at = slice(r * PIECE, (r + 1) * PIECE)
        rows = pl.ds(pl.multiple_of(core * HALF + r * PIECE, PIECE), PIECE)
        e_own, e_other = two(ends_own, r), two(ends_other, r)
        chips = in_b[at, :]
        later[rows, :] = jnp.where(first, e_other * chips + grad_other[at, :], chips)
        back_b[at, :] = jnp.where(first, chips, e_own * chips + grad[rows, :])
    back[1].start()
    back[0].wait()
    back[1].wait()

    db_out[...] = jnp.zeros_like(db_out)
    dc_out[...] = jnp.zeros_like(dc_out)

    def after(g, end):
        rows = pl.ds(pl.multiple_of(g * GROUP_ROWS, GROUP_ROWS), GROUP_ROWS)
        heads = pl.ds(pl.multiple_of(g * GROUP, GROUP), GROUP)
        a, l = carried[rows, :], later[rows, :]
        a_hi, a_lo = split(a)
        l_hi, l_lo = split(l)
        readout = mul_nt(a_hi, c_ref[...]) + mul_nt(a_lo, c_ref[...])
        q_part = mul_nt(l_hi, b_ref[...]) + mul_nt(l_lo, b_ref[...])
        x8, g8 = xt[rows, :].astype(F32), gt[rows, :].astype(F32)
        y0 = y_t[rows, :] + spread(grow_s[heads, :]) * readout
        tq = spread(tail_s[heads, :]) * q_part
        d0 = d_t[rows, :] + tq
        u_s[heads, :] = folded(g8 * y0, GROUP)
        v_s[heads, :] = folded(x8 * d0, GROUP)
        from_tail = folded(x8 * tq, GROUP)
        cross = folded(a * l, GROUP)
        ends = ends_own[heads, :]
        extra = jnp.sum(from_tail + ends * cross, axis=1, keepdims=True)
        lanes = lax.broadcasted_iota(jnp.int32, (GROUP, 128), 1)
        u_s[heads, :] += jnp.where(lanes == 127, jnp.broadcast_to(extra, (GROUP, 128)), 0.0)
        gains = spread(skip_s[heads, :])
        y_out[:, rows] = jnp.transpose(y0 + gains * x8).astype(BF16)
        dx_out[:, rows] = jnp.transpose(d0 + gains * g8).astype(BF16)
        db_out[...] += mul(txn_hi[:, rows], l_hi) + mul(txn_hi[:, rows], l_lo) + mul(txn_lo[:, rows], l_hi)
        dc_out[...] += mul(egn_hi[:, rows], a_hi) + mul(egn_hi[:, rows], a_lo) + mul(egn_lo[:, rows], a_hi)
        return end

    lax.fori_loop(0, GROUPS, after, 0)

    u, v = u_s[...], v_s[...]
    step = step_s[...]
    rate_gain = jnp.exp(rate)
    dlog = lane_sums(u - v, True)
    dstep = v / step - rate_gain * dlog
    draw = dstep / (1.0 + jnp.exp(-z))
    dt_out[...] = draw
    rate_sum = jnp.sum(dlog * (-rate_gain * step), axis=1, keepdims=True)
    bias_sum = jnp.sum(draw, axis=1, keepdims=True)
    skip_sum = jnp.sum(sk_s[...], axis=1, keepdims=True)
    lanes = lax.broadcasted_iota(jnp.int32, square, 1)
    share[...] = jnp.where(lanes == 0, rate_sum, jnp.where(lanes == 1, bias_sum, jnp.where(lanes == 2, skip_sum, 0.0)))
    own8 = pl.ds(pl.multiple_of(dp * 8, 8), 8)
    share_got[dp] = share[own8, :]
    sends = []
    for k in range(1, n_dp):
        peer = lax.rem(dp + k, n_dp)
        copy = to(
            share.at[pl.ds(pl.multiple_of(peer * 8, 8), 8)], share_got.at[dp], share_ss.at[k], share_rs.at[k], {"dp": peer}
        )
        copy.start()
        sends.append(copy)

    g_hi, g_lo = split(dgram_t[...])
    db_out[...] += mul(g_hi, c_ref[...]) + mul(g_lo, c_ref[...])
    t_hi, t_lo = split(jnp.transpose(dgram_t[...]))
    dc_out[...] += mul(t_hi, b_ref[...]) + mul(t_lo, b_ref[...])

    for copy in sends:
        copy.wait()
    summed = share_got[0]
    for k in range(1, n_dp):
        summed = summed + share_got[k]
    total[...] = summed
    total_got[me] = summed
    sends = []
    for k in range(1, n_ctx):
        copy = to(total, total_got.at[me], total_ss.at[k], total_rs.at[k], {"ctx": lax.rem(me + k, n_ctx)})
        copy.start()
        sends.append(copy)
    for copy in sends:
        copy.wait()
    summed = total_got[0]
    for k in range(1, n_ctx):
        summed = summed + total_got[k]
    lines = jnp.transpose(jnp.concatenate([summed] * 16, axis=0))
    rate_out[...] = lines[0:1, 0:8]
    bias_out[...] = lines[1:2, 0:8]
    skip_out[...] = lines[2:3, 0:8]


def local(x, b, c, raw, rate, bias, skip, g):
    n_dp, n_ctx = lax.axis_size("dp"), lax.axis_size("ctx")
    vmem = pl.BlockSpec(memory_space=pltpu.VMEM)
    smem = pl.BlockSpec(memory_space=pltpu.SMEM)
    wide = (ROWS, 128)
    half = (HALF, 128)
    small = (HEADS, 128)

    def buf(shape, dtype=F32):
        return pltpu.VMEM(shape, dtype)

    scratch = [
        buf(wide, BF16), buf(wide, BF16), buf((TOKENS, TOKENS)), buf((n_dp, 8, 128)),
        *[buf(small)] * 5, buf((GROUPS, TOKENS, GROUP)), buf((GROUPS, TOKENS, GROUP)),
        *[buf(wide, BF16)] * 4, *[buf((TOKENS, ROWS), BF16)] * 4,
        buf(small), buf(small), buf(wide), buf(wide), buf(half), buf(half),
        buf((CHIPS, PIECE + 8, 128)), buf((CHIPS, PIECE, 128)), buf((CHIPS, PIECE + 8, 128)), buf((CHIPS, PIECE, 128)),
        buf((CHIPS, PIECE, 128)), buf((CHIPS, PIECE, 128)), buf(half), buf(half), buf(half), buf(half), buf(wide), buf(wide),
        buf(wide), buf(wide), buf((TOKENS, TOKENS)), buf(small), buf(small), buf(small),
        buf(small), buf((n_dp, 8, 128)), buf((8, 128)), buf((n_ctx, 8, 128)),
        *[pltpu.SemaphoreType.DMA((n_dp,))] * 2, *[pltpu.SemaphoreType.DMA((3,))] * 2,
        *[pltpu.SemaphoreType.DMA((CHIPS,))] * 8, *[pltpu.SemaphoreType.DMA((2,))] * 2,
        *[pltpu.SemaphoreType.DMA((n_dp,))] * 2, *[pltpu.SemaphoreType.DMA((n_ctx,))] * 2,
    ]
    shapes = [
        jax.ShapeDtypeStruct((TOKENS, ROWS), BF16), jax.ShapeDtypeStruct((TOKENS, ROWS), BF16),
        jax.ShapeDtypeStruct((TOKENS, ENTRIES), F32), jax.ShapeDtypeStruct((TOKENS, ENTRIES), F32),
        jax.ShapeDtypeStruct((HEADS, TOKENS), F32),
        *[jax.ShapeDtypeStruct((1, 8), F32)] * 3,
    ]
    y, dx, db, dc, dt, dr, dbias, dskip = pl.pallas_call(
        kernel,
        out_shape=shapes,
        in_specs=[vmem, vmem, vmem, vmem, smem, smem, smem, vmem],
        out_specs=[vmem] * 8,
        scratch_shapes=scratch,
        compiler_params=pltpu.CompilerParams(collective_id=0, has_side_effects=True, vmem_limit_bytes=48 << 20),
        name="layer",
    )(x[0], b[0], c[0], raw[0], rate, bias, skip, g[0])
    return y[None], dx[None], db[None], dc[None], dt[None], dr.reshape(8), dbias.reshape(8), dskip.reshape(8)


def solution(mesh):
    tokens = P("dp", "ctx", None)
    strides = P("dp", None, "ctx")
    owned = P("dp")
    return jax.shard_map(
        local,
        mesh=mesh,
        in_specs=(tokens, tokens, tokens, strides, owned, owned, owned, tokens),
        out_specs=(tokens, tokens, tokens, tokens, strides, owned, owned, owned),
        check_vma=False,
    )
```

time: 377 us -> 78.8 us (0.21)
  waiting for transfers between devices: 201 us -> 0 us
  Pallas kernels: 0 us -> 67.7 us
  blocking collectives: 50.9 us -> 0 us
  other arithmetic: 37.9 us -> 0 us
  starting transfers between devices: 29 us -> 0 us
  matrix products: 28.2 us -> 0 us
  between operations: 15.9 us -> 0.68 us
    all_gather x6 -> x0, waiting for transfers between devices: 191 us -> none  [entering(): pieces = jax.tree.map(lambda part: lax.all_gather(part, axis), subtotal)]
    pallas_call x0 -> x1, Pallas kernels: none -> 67.7 us  [local(): pl.pallas_call(kernel, out_shape=shapes, in_specs=[vmem, vmem, vmem, vmem...]
    all_gather x3 -> x0, blocking collectives: 34.2 us -> none  [the longest x1 20.4 us: rows_first(): result = lax.all_gather(both, axis, axis=0, tiled=True)]
    all_to_all x4 -> x0, starting transfers between devices: 28.7 us -> none  [the longest x3 20.1 us: summed_on_arrival(): lax.all_to_all(split_up(array, dim, devices), axis, 0, 0, tiled=True)]
    dot_general x12 -> x0, matrix products: 28.2 us -> none  [the longest x3 14.2 us: local_part(): inner = jnp.einsum('hts,shp->thp', weights, xg3, precision=maximal_accuracy)]
    add x6 -> x0, other arithmetic: 19.7 us -> none  [the longest x5 19.6 us: combine(): later[0][:, None, None] * earlier[1] + later[1]]
    unnamed x2 -> x0, blocking collectives: 16.7 us -> none
    reduce_sum x9 -> x0, other arithmetic: 12 us -> none  [the longest x1 8.6 us: local(): end_grad = jnp.sum(later * carried, axis=(1, 2))]
  transfers between devices with their start and end apart: 10 -> 0, of which waited for: 8 -> 0; matrix products, arithmetic and copies ran while one was open for 9% -> 0% of each run, Pallas kernels for 0% -> 0%
where the time goes in v1:
time: 78.8 us; the launch traced here: 78.4 us
  Pallas kernels  67.7 us (86%)
  local copies, waits for them, and re-layouts  10 us (13%)
    pallas_call x1, Pallas kernels, local(): pl.pallas_call(kernel, out_shape=shapes, in_specs=[vmem, vmem, vmem, vmem...  67.7 us
    unnamed x24, local copies, waits for them, and re-layouts  10 us

profile of v1, /device:TPU:1, one launch (start us, length us, event | category | flops | bytes accessed | tf_op | source)
XLA Modules:
  0.0 78.4 jit_solution(7399394073075799012)
XLA Ops:
  0.6 0.0 copy-start.5
  0.6 0.0 copy-start.6
  0.7 0.0 copy-start.7
  0.7 0.6 copy-done.5
  1.3 0.0 copy-done.6
  1.3 0.0 copy-done.7
  1.3 0.0 copy-start
  1.3 1.0 %copy-done = bf16[1,128,2048]{2,1,0:T(8,128)(2,1)S(1)} copy-done((bf16[1,128,2048]{2,1,0:T(8,128)(2,1)S(1)}, bf16[1,128,2048]{2,1,0:T(8,128)(2,1)}, u32[]{:S(2)}) %copy-start) | copy-done | bytes 524312
  2.4 0.0 copy-start.1
  2.4 1.0 %copy-done.1 = bf16[1,128,2048]{2,1,0:T(8,128)(2,1)S(1)} copy-done((bf16[1,128,2048]{2,1,0:T(8,128)(2,1)S(1)}, bf16[1,128,2048]{2,1,0:T(8,128)(2,1)}, u32[]{:S(2)}) %copy-start.1) | copy-done | bytes 524312
  3.4 0.0 copy-start.2
  3.4 0.8 copy-done.2
  4.2 0.0 copy-start.3
  4.2 0.8 copy-done.3
  4.9 0.0 copy-start.4
  4.9 0.8 copy-done.4
  5.7 67.7 %layer.1 = (bf16[128,2048]{1,0:T(8,128)(2,1)S(1)}, bf16[128,2048]{1,0:T(8,128)(2,1)S(1)}, f32[128,128]{1,0:T(8,128)S(1)}, f32[128,128]{1,0:T(8,128)S(1)}, f32[64...) custom-call(bf16[128,2048]{1,0:T(8,128)(2,1)S(1)} %bitcast.13, ...), custom_call_target="tpu_custom_call" | custom-call | tf_op jit(solution)/shard_map/layer/pallas_call | solution.py:442
  73.4 0.8 %copy.24 = bf16[1,128,2048]{2,1,0:T(8,128)(2,1)} copy(bf16[1,128,2048]{2,1,0:T(8,128)(2,1)S(1)} %bitcast.16) | data formatting | bytes 1048576
  74.2 0.8 %copy.25 = bf16[1,128,2048]{2,1,0:T(8,128)(2,1)} copy(bf16[1,128,2048]{2,1,0:T(8,128)(2,1)S(1)} %bitcast.15) | data formatting | bytes 1048576
  75.0 0.6 copy.26
  75.6 0.6 copy.27
  76.3 0.6 copy.28
  76.9 0.5 copy.29
  77.4 0.5 copy.30
  77.9 0.5 copy.31
Async XLA Ops:
  0.6 0.7 copy-start.5
  0.6 0.7 copy-start.6
  0.7 0.7 copy-start.7
  1.3 1.0 %copy-start = (bf16[1,128,2048]{2,1,0:T(8,128)(2,1)S(1)}, bf16[1,128,2048]{2,1,0:T(8,128)(2,1)}, u32[]{:S(2)}) copy-start(bf16[1,128,2048]{2,1,0:T(8,128)(2,1)} %param.8) | copy-start | bytes 1572868
  2.4 1.0 %copy-start.1 = (bf16[1,128,2048]{2,1,0:T(8,128)(2,1)S(1)}, bf16[1,128,2048]{2,1,0:T(8,128)(2,1)}, u32[]{:S(2)}) copy-start(bf16[1,128,2048]{2,1,0:T(8,128)(2,1)} %param.15) | copy-start | bytes 1572868
  3.4 0.8 copy-start.2
  4.2 0.8 copy-start.3
  4.9 0.8 copy-start.4

commit v2 on v1

v2 whole, which is shorter than its diff:
```python
import jax
import jax.numpy as jnp
from jax import lax
from jax.experimental import pallas as pl
from jax.experimental.pallas import tpu as pltpu
from jax.sharding import PartitionSpec as P

MESH = pl.DeviceIdType.MESH
F32, BF16 = jnp.float32, jnp.bfloat16

TOKENS = 128
HEADS = 64
WIDTH = 32
ENTRIES = 128
ROWS = HEADS * WIDTH
HALF = ROWS // 2
GROUP = 8
GROUP_ROWS = GROUP * WIDTH
GROUPS = HEADS // GROUP
CHIPS = 16
PIECE = HALF // CHIPS


def split(value):
    high = value.astype(BF16)
    return high, (value - high.astype(F32)).astype(BF16)


def mul(a, b):
    return jnp.dot(a, b, preferred_element_type=F32)


def mul_nt(a, b):
    return lax.dot_general(a, b, (((1,), (1,)), ((), ())), preferred_element_type=F32)


def spread(rows, width=WIDTH):
    count = rows.shape[0]
    parts = [jnp.broadcast_to(rows[k : k + 1, :], (width, rows.shape[1])) for k in range(count)]
    return jnp.concatenate(parts, axis=0)


def folded(value, count):
    return jnp.sum(value.reshape(count, WIDTH, value.shape[1]), axis=1)


def lane_sums(value, reverse):
    lanes = lax.broadcasted_iota(jnp.int32, value.shape, 1)
    size = value.shape[1]
    shift = 1
    while shift < size:
        if reverse:
            moved = jnp.where(lanes < size - shift, pltpu.roll(value, size - shift, 1), 0.0)
        else:
            moved = jnp.where(lanes >= shift, pltpu.roll(value, shift, 1), 0.0)
        value = value + moved
        shift *= 2
    return value
SPLIT = (1, 3, 5)


def layer(
    x_hbm, b_hbm, c_hbm, raw_hbm, rate_hbm, bias_hbm, skip_hbm, g_hbm,
    y_hbm, dx_hbm, db_hbm, dc_hbm, dt_hbm, total_got,
    y_out, dx_out, db_out, dc_out, dt_out,
    x_ref, b_ref, c_ref, raw_ref, g_ref, rate_ref, bias_ref, skip_ref,
    xt, gt, gram_t, par_recv, cum_s, step_s, tail_s, grow_s, skip_s, cum_col, step_col,
    tx_hi, tx_lo, eg_hi, eg_lo, txn_hi, txn_lo, egn_hi, egn_lo,
    ends_own, ends_other, state, grad, state_other, grad_other,
    tot_f, tot_b, got_f, got_b, pre_f, pre_b, in_f, in_b, back_f, back_b, carried, later,
    y_t, d_t, dgram_t, u_s, v_s, sk_s, share, share_got, total,
    in_sem, out_sem, par_ss, par_rs, pair_ss, pair_rs, f1_ss, f1_rs, b1_ss, b1_rs, f2_ss, f2_rs, b2_ss, b2_rs,
    back_ss, back_rs, share_ss, share_rs, total_ss, total_rs,
):
    me = lax.axis_index("ctx")
    dp = lax.axis_index("dp")
    n_dp = lax.axis_size("dp")
    n_ctx = lax.axis_size("ctx")
    core = lax.rem(me, 2)
    chip = me // 2
    partner = chip * 2 + 1 - core
    first = core == 0

    def to(src, dst, ss, rs, where):
        return pltpu.make_async_remote_copy(src, dst, ss, rs, device_id=where, device_id_type=MESH)

    barrier = pltpu.get_barrier_semaphore()
    for k in range(1, n_dp):
        pl.semaphore_signal(barrier, 1, device_id={"dp": lax.rem(dp + k, n_dp)}, device_id_type=MESH)
    for k in range(1, n_ctx):
        pl.semaphore_signal(barrier, 1, device_id={"ctx": lax.rem(me + k, n_ctx)}, device_id_type=MESH)

    loads = [
        pltpu.make_async_copy(src, dst, in_sem.at[k])
        for k, (src, dst) in enumerate(
            (
                (rate_hbm, rate_ref), (bias_hbm, bias_ref), (skip_hbm, skip_ref), (raw_hbm, raw_ref),
                (x_hbm, x_ref), (b_hbm, b_ref), (g_hbm, g_ref), (c_hbm, c_ref),
            )
        )
    ]
    for copy in loads:
        copy.start()
    for copy in loads[:3]:
        copy.wait()

    lanes8 = lax.broadcasted_iota(jnp.int32, (8, 128), 1)
    rows8 = lax.broadcasted_iota(jnp.int32, (8, 128), 0)
    tile = jnp.zeros((8, 128), F32)
    for row, ref in enumerate((rate_ref, bias_ref, skip_ref)):
        for j in range(8):
            here = jnp.logical_and(rows8 == row, lanes8 == dp * 8 + j)
            tile = jnp.where(here, ref[j], tile)
    par_recv[dp] = tile

    pl.semaphore_wait(barrier, n_dp + n_ctx - 2)

    def to_all(src, dst, ss, rs, axis, size, index):
        for k in range(1, size):
            to(src(k), dst, ss.at[0], rs.at[0], {axis: lax.rem(index + k, size)}).start()

    to_all(lambda k: par_recv.at[dp], par_recv.at[dp], par_ss, par_rs, "dp", n_dp, dp)

    for copy in loads[3:]:
        copy.wait()
    for k in range(GROUPS):
        at = slice(k * GROUP_ROWS, (k + 1) * GROUP_ROWS)
        xt[at, :] = jnp.transpose(x_ref[:, at].astype(F32)).astype(BF16)
        gt[at, :] = jnp.transpose(g_ref[:, at].astype(F32)).astype(BF16)
    gram_t[...] = mul_nt(b_ref[...], c_ref[...])

    seven = pl.ds(0, n_dp - 1)
    to(par_recv.at[seven], par_recv.at[seven], par_ss.at[0], par_rs.at[0], {"dp": dp}).wait()

    params = par_recv[0]
    for k in range(1, n_dp):
        params = params + par_recv[k]
    columns = jnp.transpose(jnp.concatenate([params] * 16, axis=0))[:HEADS, :]
    square = (HEADS, 128)
    rate = jnp.broadcast_to(columns[:, 0:1], square)
    bias = jnp.broadcast_to(columns[:, 1:2], square)
    skip_s[...] = jnp.broadcast_to(columns[:, 2:3], square)
    z = raw_ref[...] + bias
    step = jnp.maximum(z, 0.0) + jnp.log1p(jnp.exp(-jnp.abs(z)))
    cum = lane_sums(-jnp.exp(rate) * step, False)
    last = jnp.broadcast_to(cum[:, 127:128], square)
    cum_s[...] = cum
    step_s[...] = step
    tail_s[...] = jnp.exp(last - cum) * step
    grow_s[...] = jnp.exp(cum)
    ends_own[...] = jnp.exp(last)

    def rows_of(g):
        return pl.ds(pl.multiple_of(g * GROUP_ROWS, GROUP_ROWS), GROUP_ROWS)

    def heads_of(g):
        return pl.ds(pl.multiple_of(g * GROUP, GROUP), GROUP)

    outs = [
        pltpu.make_async_copy(src, dst, out_sem.at[k])
        for k, (src, dst) in enumerate(
            (
                (y_out, y_hbm), (dc_out, dc_hbm), (dt_out, dt_hbm), (dx_out, dx_hbm), (db_out, db_hbm),
                (total, total_got.at[me]),
            )
        )
    ]

    def states(g):
        rows, heads = rows_of(g), heads_of(g)
        hi, lo = split(xt[rows, :].astype(F32) * spread(tail_s[heads, :]))
        tx_hi[rows, :] = hi
        tx_lo[rows, :] = lo
        state[rows, :] = mul(hi, b_ref[...]) + mul(lo, b_ref[...])

    def grads(g):
        rows, heads = rows_of(g), heads_of(g)
        hi, lo = split(gt[rows, :].astype(F32) * spread(grow_s[heads, :]))
        eg_hi[rows, :] = hi
        eg_lo[rows, :] = lo
        grad[rows, :] = mul(hi, c_ref[...]) + mul(lo, c_ref[...])

    mine = pl.ds(pl.multiple_of(core * HALF, HALF), HALF)
    theirs = pl.ds(pl.multiple_of((1 - core) * HALF, HALF), HALF)
    there = {"ctx": partner}
    half_groups = GROUPS // 2
    base = core * (HEADS // 2)

    def row_of(ref, head):
        return jnp.broadcast_to(ref[pl.ds(head, 1), :], (WIDTH, 128))

    def two(ref, r):
        return jnp.concatenate([row_of(ref, base + 2 * r), row_of(ref, base + 2 * r + 1)], axis=0)

    def piece_rows(r):
        return pl.ds(pl.multiple_of(core * HALF + r * PIECE, PIECE), PIECE)

    def chip_of(k):
        return lax.rem(chip + k, CHIPS)

    def chip_id(k):
        return {"ctx": chip_of(k) * 2 + core}

    spot = pl.ds(pl.multiple_of(chip * PIECE, PIECE), PIECE)
    others = pl.ds(0, CHIPS - 1)
    most = pl.ds(0, HALF - PIECE)

    def out_pieces(src, dst, ss, rs):
        for k in range(1, CHIPS):
            to(src.at[chip_of(k)], dst, ss.at[0], rs.at[0], chip_id(k)).start()

    def all_pieces(src, ss, rs):
        return to(src.at[others], src.at[others], ss.at[0], rs.at[0], there)

    ends_pair = to(ends_own, ends_other, pair_ss.at[0], pair_rs.at[0], there)
    state_pair = to(state.at[theirs], state_other, pair_ss.at[1], pair_rs.at[1], there)
    grad_pair = to(grad.at[theirs], grad_other, pair_ss.at[2], pair_rs.at[2], there)
    ends_pair.start()
    for k in range(half_groups):
        states((1 - core) * half_groups + k)
    state_pair.start()
    for k in range(half_groups):
        states(core * half_groups + k)

    ends_pair.wait()
    state_pair.wait()
    for r in range(CHIPS):
        e_own, e_other = two(ends_own, r), two(ends_other, r)
        own, other = state[piece_rows(r), :], state_other[r * PIECE : (r + 1) * PIECE, :]
        tot_f[r, 0:PIECE, :] = jnp.where(first, e_other * own + other, own + e_own * other)
        decay = jnp.concatenate(
            [ends_own[pl.ds(base + 2 * r + k, 1), :] * ends_other[pl.ds(base + 2 * r + k, 1), :] for k in range(2)] * 4, axis=0
        )
        tot_f[r, PIECE : PIECE + 8, :] = decay
    got_f[chip] = tot_f[chip]
    out_pieces(tot_f, got_f.at[chip], f1_ss, f1_rs)

    for k in range(half_groups):
        grads((1 - core) * half_groups + k)
    grad_pair.start()
    for k in range(half_groups):
        grads(core * half_groups + k)

    def padded(value):
        return jnp.transpose(jnp.concatenate([value, value], axis=0))

    cum_t, step_t = padded(cum_s[...]), padded(step_s[...])
    for k in range(GROUPS):
        cum_col[k] = cum_t[:, k * GROUP : (k + 1) * GROUP]
        step_col[k] = step_t[:, k * GROUP : (k + 1) * GROUP]
    dgram_t[...] = jnp.zeros_like(dgram_t)

    def within(g, _):
        rows, heads = rows_of(g), heads_of(g)
        cum8, cumc, stepc = cum_s[heads, :], cum_col[g], step_col[g]
        xt8, gt8 = xt[rows, :], gt[rows, :]
        above = lax.broadcasted_iota(jnp.int32, (TOKENS, TOKENS), 0) <= lax.broadcasted_iota(
            jnp.int32, (TOKENS, TOKENS), 1
        )
        gram = gram_t[...]
        acc = dgram_t[...]
        none = jnp.zeros((WIDTH, TOKENS), BF16)
        for quad in range(2):
            xq = x_ref[:, pl.ds(pl.multiple_of(g * GROUP_ROWS + quad * 128, 128), 128)]
            for j in range(4):
                k = quad * 4 + j
                at = slice(k * WIDTH, (k + 1) * WIDTH)
                g_rows = gt8[at, :]
                weights_g = jnp.concatenate([g_rows if i == j else none for i in range(4)], axis=0)
                dw = mul(xq, weights_g)
                diff = jnp.broadcast_to(cum8[k : k + 1, :], (TOKENS, TOKENS)) - jnp.broadcast_to(
                    cumc[:, k : k + 1], (TOKENS, TOKENS)
                )
                seg = jnp.exp(jnp.where(above, diff, -1e30))
                factor = seg * jnp.broadcast_to(stepc[:, k : k + 1], (TOKENS, TOKENS))
                acc = acc + dw * factor
                hi, lo = split(gram * factor)
                inner = mul(xt8[at, :], hi) + mul(xt8[at, :], lo)
                back = mul_nt(g_rows, hi) + mul_nt(g_rows, lo)
                out = pl.ds(pl.multiple_of(g * GROUP_ROWS + k * WIDTH, WIDTH), WIDTH)
                y_t[out, :] = inner
                d_t[out, :] = back
        dgram_t[...] = acc
        sk_s[heads, :] = folded(xt8.astype(F32) * gt8.astype(F32), GROUP)
        return 0

    def turn_of(pairs):
        def turn(k, _):
            rows = pl.ds(pl.multiple_of(k * 128, 128), 128)
            for src, dst in pairs:
                dst[:, rows] = jnp.transpose(src[rows, :].astype(F32)).astype(BF16)
            return 0

        lax.fori_loop(0, ROWS // 128, turn, 0)

    grad_pair.wait()
    for r in range(CHIPS):
        e_own, e_other = two(ends_own, r), two(ends_other, r)
        own, other = grad[piece_rows(r), :], grad_other[r * PIECE : (r + 1) * PIECE, :]
        tot_b[r] = jnp.where(first, own + e_own * other, e_other * own + other)
    got_b[chip] = tot_b[chip]
    lax.fori_loop(0, SPLIT[0], within, 0)
    f1_all = all_pieces(tot_f, f1_ss, f1_rs)
    f1_all.wait_send()
    out_pieces(tot_b, got_b.at[chip], b1_ss, b1_rs)

    lax.fori_loop(SPLIT[0], SPLIT[1], within, 0)

    def decay_of(q):
        return jnp.concatenate(
            [jnp.broadcast_to(got_f[q, PIECE + k : PIECE + k + 1, :], (WIDTH, 128)) for k in range(2)], axis=0
        )

    f1_all.wait_recv()
    run = jnp.zeros((PIECE, 128), F32)
    for q in range(CHIPS):
        pre_f[q] = run
        run = decay_of(q) * run + got_f[q, 0:PIECE, :]
    in_f[spot, :] = pre_f[chip]
    b1_all = all_pieces(tot_b, b1_ss, b1_rs)
    b1_all.wait_send()
    out_pieces(pre_f, in_f.at[spot], f2_ss, f2_rs)

    lax.fori_loop(SPLIT[1], SPLIT[2], within, 0)

    b1_all.wait_recv()
    run = jnp.zeros((PIECE, 128), F32)
    for q in reversed(range(CHIPS)):
        pre_b[q] = run
        run = decay_of(q) * run + got_b[q]
    in_b[spot, :] = pre_b[chip]
    all_pieces(pre_f, f2_ss, f2_rs).wait_send()
    out_pieces(pre_b, in_b.at[spot], b2_ss, b2_rs)

    lax.fori_loop(SPLIT[2], GROUPS, within, 0)

    back_f_pair = to(back_f, carried.at[mine], back_ss.at[0], back_rs.at[0], there)
    back_b_pair = to(back_b, later.at[mine], back_ss.at[1], back_rs.at[1], there)
    to(in_f.at[most], in_f.at[most], f2_ss.at[0], f2_rs.at[0], there).wait_recv()
    for r in range(CHIPS):
        at = slice(r * PIECE, (r + 1) * PIECE)
        e_own, e_other = two(ends_own, r), two(ends_other, r)
        chips = in_f[at, :]
        carried[piece_rows(r), :] = jnp.where(first, chips, e_other * chips + state_other[at, :])
        back_f[at, :] = jnp.where(first, e_own * chips + state[piece_rows(r), :], chips)
    back_f_pair.start()
    turn_of(((eg_hi, egn_hi), (eg_lo, egn_lo)))
    back_f_pair.wait()

    dc_out[...] = jnp.zeros_like(dc_out)
    db_out[...] = jnp.zeros_like(db_out)

    def after_f(g, _):
        rows, heads = rows_of(g), heads_of(g)
        a_hi, a_lo = split(carried[rows, :])
        readout = mul_nt(a_hi, c_ref[...]) + mul_nt(a_lo, c_ref[...])
        x8, g8 = xt[rows, :].astype(F32), gt[rows, :].astype(F32)
        y0 = y_t[rows, :] + spread(grow_s[heads, :]) * readout
        u_s[heads, :] = folded(g8 * y0, GROUP)
        y_out[:, rows] = jnp.transpose(y0 + spread(skip_s[heads, :]) * x8).astype(BF16)
        dc_out[...] += mul(egn_hi[:, rows], a_hi) + mul(egn_hi[:, rows], a_lo) + mul(egn_lo[:, rows], a_hi)
        return 0

    lax.fori_loop(0, GROUPS, after_f, 0)
    turn_of(((tx_hi, txn_hi), (tx_lo, txn_lo)))
    g_hi, g_lo = split(dgram_t[...])
    db_out[...] += mul(g_hi, c_ref[...]) + mul(g_lo, c_ref[...])
    t_hi, t_lo = split(jnp.transpose(dgram_t[...]))
    dc_out[...] += mul(t_hi, b_ref[...]) + mul(t_lo, b_ref[...])
    outs[0].start()
    outs[1].start()

    to(in_b.at[most], in_b.at[most], b2_ss.at[0], b2_rs.at[0], there).wait_recv()
    for r in range(CHIPS):
        at = slice(r * PIECE, (r + 1) * PIECE)
        e_own, e_other = two(ends_own, r), two(ends_other, r)
        chips = in_b[at, :]
        later[piece_rows(r), :] = jnp.where(first, e_other * chips + grad_other[at, :], chips)
        back_b[at, :] = jnp.where(first, chips, e_own * chips + grad[piece_rows(r), :])
    back_b_pair.start()

    def after_b(g, _):
        rows, heads = rows_of(g), heads_of(g)
        l = later[rows, :]
        l_hi, l_lo = split(l)
        tq = spread(tail_s[heads, :]) * (mul_nt(l_hi, b_ref[...]) + mul_nt(l_lo, b_ref[...]))
        x8 = xt[rows, :].astype(F32)
        d0 = d_t[rows, :] + tq
        d_t[rows, :] = d0
        v_s[heads, :] = folded(x8 * d0, GROUP)
        extra = folded(x8 * tq, GROUP) + ends_own[heads, :] * folded(carried[rows, :] * l, GROUP)
        extra = jnp.broadcast_to(jnp.sum(extra, axis=1, keepdims=True), (GROUP, 128))
        lanes = lax.broadcasted_iota(jnp.int32, (GROUP, 128), 1)
        u_s[heads, :] += jnp.where(lanes == 127, extra, 0.0)
        return 0

    lax.fori_loop(core * half_groups, (core + 1) * half_groups, after_b, 0)
    back_b_pair.wait()
    lax.fori_loop((1 - core) * half_groups, (2 - core) * half_groups, after_b, 0)

    u, v = u_s[...], v_s[...]
    step = step_s[...]
    rate_gain = jnp.exp(rate)
    dlog = lane_sums(u - v, True)
    dstep = v / step - rate_gain * dlog
    draw = dstep / (1.0 + jnp.exp(-z))
    dt_out[...] = draw
    outs[2].start()
    rate_sum = jnp.sum(dlog * (-rate_gain * step), axis=1, keepdims=True)
    bias_sum = jnp.sum(draw, axis=1, keepdims=True)
    skip_sum = jnp.sum(sk_s[...], axis=1, keepdims=True)
    lanes = lax.broadcasted_iota(jnp.int32, square, 1)
    share[...] = jnp.where(lanes == 0, rate_sum, jnp.where(lanes == 1, bias_sum, jnp.where(lanes == 2, skip_sum, 0.0)))

    def eight(d):
        return pl.ds(pl.multiple_of(d * 8, 8), 8)

    share_got[dp] = share[eight(dp), :]
    to_all(lambda k: share.at[eight(lax.rem(dp + k, n_dp))], share_got.at[dp], share_ss, share_rs, "dp", n_dp, dp)

    def finish(g, _):
        rows, heads = rows_of(g), heads_of(g)
        g8 = gt[rows, :].astype(F32)
        dx_out[:, rows] = jnp.transpose(d_t[rows, :] + spread(skip_s[heads, :]) * g8).astype(BF16)
        l_hi, l_lo = split(later[rows, :])
        db_out[...] += mul(txn_hi[:, rows], l_hi) + mul(txn_hi[:, rows], l_lo) + mul(txn_lo[:, rows], l_hi)
        return 0

    lax.fori_loop(0, GROUPS, finish, 0)
    outs[3].start()
    outs[4].start()

    to(share_got.at[seven], share_got.at[seven], share_ss.at[0], share_rs.at[0], {"dp": dp}).wait()
    summed = share_got[0]
    for k in range(1, n_dp):
        summed = summed + share_got[k]
    total[...] = summed
    outs[5].start()
    to_all(lambda k: total, total_got.at[me], total_ss, total_rs, "ctx", n_ctx, me)
    all_pieces(pre_b, b2_ss, b2_rs).wait_send()
    for copy in outs:
        copy.wait()
    last31 = pl.ds(0, n_ctx - 1)
    to(total_got.at[last31], total_got.at[last31], total_ss.at[0], total_rs.at[0], {"ctx": me}).wait()


def write(*refs):
    sources, targets, buffers, lines, in_sem, out_sem = refs[:6], refs[6:14], refs[14:20], refs[20], refs[21], refs[22]
    loads = [pltpu.make_async_copy(src, dst, in_sem.at[k]) for k, (src, dst) in enumerate(zip(sources, buffers))]
    loads = loads[5:] + loads[:5]
    for copy in loads:
        copy.start()
    kept = [*buffers[:5], lines.at[0], lines.at[1], lines.at[2]]
    stores = [pltpu.make_async_copy(src, dst, out_sem.at[k]) for k, (src, dst) in enumerate(zip(kept, targets))]
    loads[0].wait()
    totals = buffers[5]
    summed = totals[0]
    for k in range(1, totals.shape[0]):
        summed = summed + totals[k]
    turned = jnp.transpose(jnp.concatenate([summed] * 16, axis=0))
    for k in range(3):
        lines[k] = turned[k : k + 1, 0:8]
        stores[5 + k].start()
    for k in range(5):
        loads[1 + k].wait()
        stores[k].start()
    for copy in stores:
        copy.wait()


def local(x, b, c, raw, rate, bias, skip, g):
    n_dp, n_ctx = lax.axis_size("dp"), lax.axis_size("ctx")
    vmem = pl.BlockSpec(memory_space=pltpu.VMEM)
    hbm = pl.BlockSpec(memory_space=pltpu.HBM)
    wide = (ROWS, 128)
    half = (HALF, 128)
    small = (HEADS, 128)
    piece = (CHIPS, PIECE, 128)
    longer = (CHIPS, PIECE + 8, 128)

    def buf(shape, dtype=F32):
        return pltpu.VMEM(shape, dtype)

    def sems(count):
        return pltpu.SemaphoreType.DMA((count,))

    landing = [
        buf((TOKENS, ROWS), BF16), buf((TOKENS, ROWS), BF16), buf((TOKENS, ENTRIES)), buf((TOKENS, ENTRIES)), buf(small),
        buf((n_ctx, 8, 128)),
    ]
    scratch = [
        *landing[:5],
        buf((TOKENS, ROWS), BF16), buf((TOKENS, ENTRIES), BF16), buf((TOKENS, ENTRIES), BF16), buf(small),
        buf((TOKENS, ROWS), BF16), *[pltpu.SMEM((8,), F32)] * 3,
        buf(wide, BF16), buf(wide, BF16), buf((TOKENS, TOKENS)), buf((n_dp, 8, 128)),
        *[buf(small)] * 5, buf((GROUPS, TOKENS, GROUP)), buf((GROUPS, TOKENS, GROUP)),
        *[buf(wide, BF16)] * 4, *[buf((TOKENS, ROWS), BF16)] * 4,
        buf(small), buf(small), buf(wide), buf(wide), buf(half), buf(half),
        buf(longer), buf(piece), buf(longer), buf(piece),
        buf(piece), buf(piece), buf(half), buf(half), buf(half), buf(half), buf(wide), buf(wide),
        buf(wide), buf(wide), buf((TOKENS, TOKENS)), buf(small), buf(small), buf(small),
        buf(small), buf((n_dp, 8, 128)), buf((8, 128)),
        sems(8), sems(6), sems(1), sems(1), sems(3), sems(3), *[sems(1)] * 8, sems(2), sems(2), *[sems(1)] * 4,
    ]
    wide_out = jax.ShapeDtypeStruct((TOKENS, ROWS), BF16)
    square_out = jax.ShapeDtypeStruct((TOKENS, ENTRIES), F32)
    dt_shape = jax.ShapeDtypeStruct((HEADS, TOKENS), F32)
    shapes = [wide_out, wide_out, square_out, square_out, dt_shape]
    results = pl.pallas_call(
        layer,
        out_shape=[*shapes, jax.ShapeDtypeStruct((n_ctx, 8, 128), F32)],
        in_specs=[hbm] * 8,
        out_specs=[hbm] * 6,
        scratch_shapes=scratch,
        compiler_params=pltpu.CompilerParams(collective_id=0, has_side_effects=True, vmem_limit_bytes=60 << 20),
        name="layer",
    )(x[0], b[0], c[0], raw[0], rate, bias, skip, g[0])
    y, dx, db, dc, dt, dr, dbias, dskip = pl.pallas_call(
        write,
        out_shape=[*shapes, *[jax.ShapeDtypeStruct((1, 8), F32)] * 3],
        in_specs=[hbm] * 6,
        out_specs=[hbm] * 8,
        scratch_shapes=[*landing, buf((3, 1, 8)), sems(6), sems(8)],
        compiler_params=pltpu.CompilerParams(vmem_limit_bytes=60 << 20),
        name="write",
    )(*results)
    return y[None], dx[None], db[None], dc[None], dt[None], dr.reshape(8), dbias.reshape(8), dskip.reshape(8)


def solution(mesh):
    tokens = P("dp", "ctx", None)
    strides = P("dp", None, "ctx")
    owned = P("dp")
    return jax.shard_map(
        local,
        mesh=mesh,
        in_specs=(tokens, tokens, tokens, strides, owned, owned, owned, tokens),
        out_specs=(tokens, tokens, tokens, tokens, strides, owned, owned, owned),
        check_vma=False,
    )
```

time: 78.8 us -> 68.6 us (0.87)
  local copies, waits for them, and re-layouts: 10 us -> 0 us
    unnamed x24 -> x0, local copies, waits for them, and re-layouts: 10 us -> none
    pallas_call x1 -> x2, Pallas kernels: 67.7 us -> 67.8 us  [the longest x1 65.6 us: local(): pl.pallas_call(layer, out_shape=[*shapes, jax.ShapeDtypeStruct((n_ctx, 8,...]
where the time goes in v2:
time: 68.6 us; the launch traced here: 68.5 us
  Pallas kernels  67.8 us (99%)
    pallas_call x1, Pallas kernels, local(): pl.pallas_call(layer, out_shape=[*shapes, jax.ShapeDtypeStruct((n_ctx, 8,...  65.6 us
    pallas_call x1, Pallas kernels, local(): pl.pallas_call(write, out_shape=[*shapes, *[jax.ShapeDtypeStruct((1, 8),...  2.25 us

profile of v2, /device:TPU:1, one launch (start us, length us, event | category | flops | bytes accessed | tf_op | source)
XLA Modules:
  0.0 68.5 jit_solution(15962661191473648112)
XLA Ops:
  0.6 65.6 %layer.1 = (bf16[128,2048]{1,0:T(8,128)(2,1)}, bf16[128,2048]{1,0:T(8,128)(2,1)}, f32[128,128]{1,0:T(8,128)}, f32[128,128]{1,0:T(8,128)}, f32[64,128]{1,0:T(8,128)}, /*index=5*/f32[32,8,128]{2,1,0:T(8,128)}) custom-call(bf16[128,2048]{1,0:T(8,128)(2,1)} %bitcast.13, bf16[128,128]{1,0:T(8,128)(2,1)} %bitcast.15, bf16[128,128]{1,0:T(8,128)(2,1)} %bitcast.16, ...), custom_call_target="tpu_custom_call" | custom-call | tf_op jit(solution)/shard_map/layer/pallas_call | solution.py:509
  66.2 2.2 %write.1 = (bf16[128,2048]{1,0:T(8,128)(2,1)}, bf16[128,2048]{1,0:T(8,128)(2,1)}, f32[128,128]{1,0:T(8,128)}, f32[128,128]{1,0:T(8,128)}, f32[64,128]{1,0:T(8,12...) custom-call(bf16[128,2048]{1,0:T(8,128)(2,1)} %get-tuple-element.22.refs_0_, ...), custom_call_target="tpu_custom_call" | custom-call | tf_op jit(solution)/shard_map/write/pallas_call | solution.py:518

commit v3 on v2

--- a/solution.py
+++ b/solution.py
@@ -65,7 +65,7 @@
     y_out, dx_out, db_out, dc_out, dt_out,
     x_ref, b_ref, c_ref, raw_ref, g_ref, rate_ref, bias_ref, skip_ref,
     xt, gt, gram_t, par_recv, cum_s, step_s, tail_s, grow_s, skip_s, cum_col, step_col,
-    tx_hi, tx_lo, eg_hi, eg_lo, txn_hi, txn_lo, egn_hi, egn_lo,
+    txn_hi, txn_lo, egn_hi, egn_lo, rate_s, bias_s, pack_own, x_own, g_own, pack_other, x_other, g_other, tail_o, grow_o,
     ends_own, ends_other, state, grad, state_other, grad_other,
     tot_f, tot_b, got_f, got_b, pre_f, pre_b, in_f, in_b, back_f, back_b, carried, later,
     y_t, d_t, dgram_t, u_s, v_s, sk_s, share, share_got, total,
@@ -121,12 +121,33 @@
 
     to_all(lambda k: par_recv.at[dp], par_recv.at[dp], par_ss, par_rs, "dp", n_dp, dp)
 
+    there = {"ctx": partner}
+    pack_pair = to(pack_own, pack_other, pair_ss.at[0], pair_rs.at[0], there)
+    x_pair = to(x_own, x_other, pair_ss.at[1], pair_rs.at[1], there)
+    g_pair = to(g_own, g_other, pair_ss.at[2], pair_rs.at[2], there)
+    half_groups = GROUPS // 2
+    heads_here = HEADS // 2
     for copy in loads[3:]:
         copy.wait()
-    for k in range(GROUPS):
-        at = slice(k * GROUP_ROWS, (k + 1) * GROUP_ROWS)
-        xt[at, :] = jnp.transpose(x_ref[:, at].astype(F32)).astype(BF16)
-        gt[at, :] = jnp.transpose(g_ref[:, at].astype(F32)).astype(BF16)
+    pack_own[0:TOKENS, :] = b_ref[...].astype(F32)
+    pack_own[TOKENS : 2 * TOKENS, :] = c_ref[...].astype(F32)
+    pack_own[2 * TOKENS :, :] = raw_ref[pl.ds(pl.multiple_of((1 - core) * heads_here, heads_here), heads_here), :]
+    pack_pair.start()
+
+    def turned(src, dst, sent, half):
+        for k in range(half_groups):
+            rows = pl.ds(pl.multiple_of(half * HALF + k * GROUP_ROWS, GROUP_ROWS), GROUP_ROWS)
+            value = jnp.transpose(src[:, rows].astype(F32))
+            dst[rows, :] = value.astype(BF16)
+            if sent is not None:
+                sent[k * GROUP_ROWS : (k + 1) * GROUP_ROWS, :] = value
+
+    turned(x_ref, xt, x_own, 1 - core)
+    x_pair.start()
+    turned(g_ref, gt, g_own, 1 - core)
+    g_pair.start()
+    turned(x_ref, xt, None, core)
+    turned(g_ref, gt, None, core)
     gram_t[...] = mul_nt(b_ref[...], c_ref[...])
 
     seven = pl.ds(0, n_dp - 1)
@@ -140,15 +161,29 @@
     rate = jnp.broadcast_to(columns[:, 0:1], square)
     bias = jnp.broadcast_to(columns[:, 1:2], square)
     skip_s[...] = jnp.broadcast_to(columns[:, 2:3], square)
-    z = raw_ref[...] + bias
-    step = jnp.maximum(z, 0.0) + jnp.log1p(jnp.exp(-jnp.abs(z)))
-    cum = lane_sums(-jnp.exp(rate) * step, False)
-    last = jnp.broadcast_to(cum[:, 127:128], square)
+    rate_s[...] = rate
+    bias_s[...] = bias
+
+    def steps_of(raw, rate, bias):
+        z = raw + bias
+        step = jnp.maximum(z, 0.0) + jnp.log1p(jnp.exp(-jnp.abs(z)))
+        cum = lane_sums(-jnp.exp(rate) * step, False)
+        return z, step, cum, jnp.broadcast_to(cum[:, 127:128], cum.shape)
+
+    z, step, cum, last = steps_of(raw_ref[...], rate, bias)
     cum_s[...] = cum
     step_s[...] = step
     tail_s[...] = jnp.exp(last - cum) * step
     grow_s[...] = jnp.exp(cum)
     ends_own[...] = jnp.exp(last)
+    here = pl.ds(pl.multiple_of(core * heads_here, heads_here), heads_here)
+    pack_pair.wait()
+    _, step_o, cum_o, last_o = steps_of(pack_other[2 * TOKENS :, :], rate_s[here, :], bias_s[here, :])
+    tail_o[...] = jnp.exp(last_o - cum_o) * step_o
+    grow_o[...] = jnp.exp(cum_o)
+    ends_other[...] = jnp.exp(last_o)
+    b_other = pack_other[0:TOKENS, :].astype(BF16)
+    c_other = pack_other[TOKENS : 2 * TOKENS, :].astype(BF16)
 
     def rows_of(g):
         return pl.ds(pl.multiple_of(g * GROUP_ROWS, GROUP_ROWS), GROUP_ROWS)
@@ -166,31 +201,15 @@
         )
     ]
 
-    def states(g):
-        rows, heads = rows_of(g), heads_of(g)
-        hi, lo = split(xt[rows, :].astype(F32) * spread(tail_s[heads, :]))
-        tx_hi[rows, :] = hi
-        tx_lo[rows, :] = lo
-        state[rows, :] = mul(hi, b_ref[...]) + mul(lo, b_ref[...])
-
-    def grads(g):
-        rows, heads = rows_of(g), heads_of(g)
-        hi, lo = split(gt[rows, :].astype(F32) * spread(grow_s[heads, :]))
-        eg_hi[rows, :] = hi
-        eg_lo[rows, :] = lo
-        grad[rows, :] = mul(hi, c_ref[...]) + mul(lo, c_ref[...])
-
     mine = pl.ds(pl.multiple_of(core * HALF, HALF), HALF)
-    theirs = pl.ds(pl.multiple_of((1 - core) * HALF, HALF), HALF)
-    there = {"ctx": partner}
-    half_groups = GROUPS // 2
     base = core * (HEADS // 2)
 
     def row_of(ref, head):
         return jnp.broadcast_to(ref[pl.ds(head, 1), :], (WIDTH, 128))
 
     def two(ref, r):
-        return jnp.concatenate([row_of(ref, base + 2 * r), row_of(ref, base + 2 * r + 1)], axis=0)
+        at = base + 2 * r if ref is ends_own else 2 * r
+        return jnp.concatenate([row_of(ref, at), row_of(ref, at + 1)], axis=0)
 
     def piece_rows(r):
         return pl.ds(pl.multiple_of(core * HALF + r * PIECE, PIECE), PIECE)
@@ -212,34 +231,57 @@
     def all_pieces(src, ss, rs):
         return to(src.at[others], src.at[others], ss.at[0], rs.at[0], there)
 
-    ends_pair = to(ends_own, ends_other, pair_ss.at[0], pair_rs.at[0], there)
-    state_pair = to(state.at[theirs], state_other, pair_ss.at[1], pair_rs.at[1], there)
-    grad_pair = to(grad.at[theirs], grad_other, pair_ss.at[2], pair_rs.at[2], there)
-    ends_pair.start()
-    for k in range(half_groups):
-        states((1 - core) * half_groups + k)
-    state_pair.start()
-    for k in range(half_groups):
-        states(core * half_groups + k)
-
-    ends_pair.wait()
-    state_pair.wait()
-    for r in range(CHIPS):
-        e_own, e_other = two(ends_own, r), two(ends_other, r)
-        own, other = state[piece_rows(r), :], state_other[r * PIECE : (r + 1) * PIECE, :]
-        tot_f[r, 0:PIECE, :] = jnp.where(first, e_other * own + other, own + e_own * other)
-        decay = jnp.concatenate(
-            [ends_own[pl.ds(base + 2 * r + k, 1), :] * ends_other[pl.ds(base + 2 * r + k, 1), :] for k in range(2)] * 4, axis=0
-        )
-        tot_f[r, PIECE : PIECE + 8, :] = decay
+    def product(rows, gains, entries):
+        hi, lo = split(rows.astype(F32) * spread(gains))
+        return mul(hi, entries) + mul(lo, entries)
+
+    row = chip // 4
+
+    def send(src, dst, ss, rs, g):
+        for j in range(4):
+            target = g * 4 + lax.rem(chip + j, 4)
+
+            @pl.when(target != chip)
+            def _():
+                to(src.at[target], dst, ss.at[0], rs.at[0], {"ctx": target * 2 + core}).start()
+
+    def totals_f(k, _):
+        g = lax.rem(row + k + 1, 4)
+        rows, heads = rows_of(core * half_groups + g), heads_of(core * half_groups + g)
+        local_rows, local_heads = rows_of(g), heads_of(g)
+        own = product(xt[rows, :], tail_s[heads, :], b_ref[...])
+        other = product(x_other[local_rows, :], tail_o[local_heads, :], b_other)
+        state[rows, :] = own
+        state_other[local_rows, :] = other
+        e_own, e_other = ends_own[heads, :], ends_other[local_heads, :]
+        both = jnp.where(first, spread(e_other) * own + other, own + spread(e_own) * other)
+        decay = e_own * e_other
+        for j in range(4):
+            tot_f[g * 4 + j, 0:PIECE, :] = both[j * PIECE : (j + 1) * PIECE, :]
+            tot_f[g * 4 + j, PIECE : PIECE + 8, :] = jnp.concatenate([decay[2 * j : 2 * j + 2, :]] * 4, axis=0)
+        send(tot_f, got_f.at[chip], f1_ss, f1_rs, g)
+        return 0
+
+    def totals_b(k, _):
+        g = lax.rem(row + k + 1, 4)
+        rows, heads = rows_of(core * half_groups + g), heads_of(core * half_groups + g)
+        local_rows, local_heads = rows_of(g), heads_of(g)
+        own = product(gt[rows, :], grow_s[heads, :], c_ref[...])
+        other = product(g_other[local_rows, :], grow_o[local_heads, :], c_other)
+        grad[rows, :] = own
+        grad_other[local_rows, :] = other
+        e_own, e_other = ends_own[heads, :], ends_other[local_heads, :]
+        both = jnp.where(first, own + spread(e_own) * other, spread(e_other) * own + other)
+        for j in range(4):
+            tot_b[g * 4 + j] = both[j * PIECE : (j + 1) * PIECE, :]
+        return 0
+
+    x_pair.wait()
+    lax.fori_loop(0, half_groups, totals_f, 0)
     got_f[chip] = tot_f[chip]
-    out_pieces(tot_f, got_f.at[chip], f1_ss, f1_rs)
-
-    for k in range(half_groups):
-        grads((1 - core) * half_groups + k)
-    grad_pair.start()
-    for k in range(half_groups):
-        grads(core * half_groups + k)
+    g_pair.wait()
+    lax.fori_loop(0, half_groups, totals_b, 0)
+    got_b[chip] = tot_b[chip]
 
     def padded(value):
         return jnp.transpose(jnp.concatenate([value, value], axis=0))
@@ -284,21 +326,16 @@
         sk_s[heads, :] = folded(xt8.astype(F32) * gt8.astype(F32), GROUP)
         return 0
 
-    def turn_of(pairs):
-        def turn(k, _):
-            rows = pl.ds(pl.multiple_of(k * 128, 128), 128)
-            for src, dst in pairs:
-                dst[:, rows] = jnp.transpose(src[rows, :].astype(F32)).astype(BF16)
+    def turn_of(src, gains, hi_out, lo_out):
+        def turn(g, _):
+            rows, heads = rows_of(g), heads_of(g)
+            hi, lo = split(jnp.transpose(src[rows, :].astype(F32) * spread(gains[heads, :])))
+            hi_out[:, rows] = hi
+            lo_out[:, rows] = lo
             return 0
 
-        lax.fori_loop(0, ROWS // 128, turn, 0)
-
-    grad_pair.wait()
-    for r in range(CHIPS):
-        e_own, e_other = two(ends_own, r), two(ends_other, r)
-        own, other = grad[piece_rows(r), :], grad_other[r * PIECE : (r + 1) * PIECE, :]
-        tot_b[r] = jnp.where(first, own + e_own * other, e_other * own + other)
-    got_b[chip] = tot_b[chip]
+        lax.fori_loop(0, GROUPS, turn, 0)
+
     lax.fori_loop(0, SPLIT[0], within, 0)
     f1_all = all_pieces(tot_f, f1_ss, f1_rs)
     f1_all.wait_send()
@@ -318,7 +355,6 @@
         run = decay_of(q) * run + got_f[q, 0:PIECE, :]
     in_f[spot, :] = pre_f[chip]
     b1_all = all_pieces(tot_b, b1_ss, b1_rs)
-    b1_all.wait_send()
     out_pieces(pre_f, in_f.at[spot], f2_ss, f2_rs)
 
     lax.fori_loop(SPLIT[1], SPLIT[2], within, 0)
@@ -344,7 +380,7 @@
         carried[piece_rows(r), :] = jnp.where(first, chips, e_other * chips + state_other[at, :])
         back_f[at, :] = jnp.where(first, e_own * chips + state[piece_rows(r), :], chips)
     back_f_pair.start()
-    turn_of(((eg_hi, egn_hi), (eg_lo, egn_lo)))
+    turn_of(gt, grow_s, egn_hi, egn_lo)
     back_f_pair.wait()
 
     dc_out[...] = jnp.zeros_like(dc_out)
@@ -362,7 +398,7 @@
         return 0
 
     lax.fori_loop(0, GROUPS, after_f, 0)
-    turn_of(((tx_hi, txn_hi), (tx_lo, txn_lo)))
+    turn_of(xt, tail_s, txn_hi, txn_lo)
     g_hi, g_lo = split(dgram_t[...])
     db_out[...] += mul(g_hi, c_ref[...]) + mul(g_lo, c_ref[...])
     t_hi, t_lo = split(jnp.transpose(dgram_t[...]))
@@ -438,6 +474,7 @@
     outs[5].start()
     to_all(lambda k: total, total_got.at[me], total_ss, total_rs, "ctx", n_ctx, me)
     all_pieces(pre_b, b2_ss, b2_rs).wait_send()
+    b1_all.wait_send()
     for copy in outs:
         copy.wait()
     last31 = pl.ds(0, n_ctx - 1)
@@ -477,6 +514,8 @@
     small = (HEADS, 128)
     piece = (CHIPS, PIECE, 128)
     longer = (CHIPS, PIECE + 8, 128)
+    few = (HEADS // 2, 128)
+    packed = (2 * TOKENS + HEADS // 2, 128)
 
     def buf(shape, dtype=F32):
         return pltpu.VMEM(shape, dtype)
@@ -494,8 +533,9 @@
         buf((TOKENS, ROWS), BF16), *[pltpu.SMEM((8,), F32)] * 3,
         buf(wide, BF16), buf(wide, BF16), buf((TOKENS, TOKENS)), buf((n_dp, 8, 128)),
         *[buf(small)] * 5, buf((GROUPS, TOKENS, GROUP)), buf((GROUPS, TOKENS, GROUP)),
-        *[buf(wide, BF16)] * 4, *[buf((TOKENS, ROWS), BF16)] * 4,
-        buf(small), buf(small), buf(wide), buf(wide), buf(half), buf(half),
+        *[buf((TOKENS, ROWS), BF16)] * 4, buf(small), buf(small),
+        buf(packed), buf(half), buf(half), buf(packed), buf(half), buf(half), buf(few), buf(few),
+        buf(small), buf(few), buf(wide), buf(wide), buf(half), buf(half),
         buf(longer), buf(piece), buf(longer), buf(piece),
         buf(piece), buf(piece), buf(half), buf(half), buf(half), buf(half), buf(wide), buf(wide),
         buf(wide), buf(wide), buf((TOKENS, TOKENS)), buf(small), buf(small), buf(small),

time: 68.6 us -> 63 us (0.918)
  Pallas kernels: 67.8 us -> 62.2 us
    pallas_call x1, Pallas kernels: 65.6 us -> 60 us  [local(): pl.pallas_call(layer, out_shape=[*shapes, jax.ShapeDtypeStruct((n_ctx, 8,...]
where the time goes in v3:
time: 63 us; the launch traced here: 62.8 us
  Pallas kernels  62.2 us (99%)
  between operations  0.64 us (1%)
    pallas_call x1, Pallas kernels, local(): pl.pallas_call(layer, out_shape=[*shapes, jax.ShapeDtypeStruct((n_ctx, 8,...  60 us
    pallas_call x1, Pallas kernels, local(): pl.pallas_call(write, out_shape=[*shapes, *[jax.ShapeDtypeStruct((1, 8),...  2.25 us

profile of v3, /device:TPU:1, one launch (start us, length us, event | category | flops | bytes accessed | tf_op | source)
XLA Modules:
  0.0 62.8 jit_solution(15536725373888149890)
XLA Ops:
  0.6 60.0 %layer.1 = (bf16[128,2048]{1,0:T(8,128)(2,1)}, bf16[128,2048]{1,0:T(8,128)(2,1)}, f32[128,128]{1,0:T(8,128)}, f32[128,128]{1,0:T(8,128)}, f32[64,128]{1,0:T(8,128)}, /*index=5*/f32[32,8,128]{2,1,0:T(8,128)}) custom-call(bf16[128,2048]{1,0:T(8,128)(2,1)} %bitcast.13, bf16[128,128]{1,0:T(8,128)(2,1)} %bitcast.15, bf16[128,128]{1,0:T(8,128)(2,1)} %bitcast.16, ...), custom_call_target="tpu_custom_call" | custom-call | tf_op jit(solution)/shard_map/layer/pallas_call | solution.py:549
  60.6 2.2 %write.1 = (bf16[128,2048]{1,0:T(8,128)(2,1)}, bf16[128,2048]{1,0:T(8,128)(2,1)}, f32[128,128]{1,0:T(8,128)}, f32[128,128]{1,0:T(8,128)}, f32[64,128]{1,0:T(8,12...) custom-call(bf16[128,2048]{1,0:T(8,128)(2,1)} %get-tuple-element.22.refs_0_, ...), custom_call_target="tpu_custom_call" | custom-call | tf_op jit(solution)/shard_map/write/pallas_call | solution.py:558

commit v4 on v3

--- a/solution.py
+++ b/solution.py
@@ -57,6 +57,7 @@
         shift *= 2
     return value
 SPLIT = (1, 3, 5)
+FAR = 1
 
 
 def layer(
@@ -68,8 +69,8 @@
     txn_hi, txn_lo, egn_hi, egn_lo, rate_s, bias_s, pack_own, x_own, g_own, pack_other, x_other, g_other, tail_o, grow_o,
     ends_own, ends_other, state, grad, state_other, grad_other,
     tot_f, tot_b, got_f, got_b, pre_f, pre_b, in_f, in_b, back_f, back_b, carried, later,
-    y_t, d_t, dgram_t, u_s, v_s, sk_s, share, share_got, total,
-    in_sem, out_sem, par_ss, par_rs, pair_ss, pair_rs, f1_ss, f1_rs, b1_ss, b1_rs, f2_ss, f2_rs, b2_ss, b2_rs,
+    y_t, d_t, dgram_t, u_s, v_s, sk_s, z_s, z_o, step_o, u_o, v_o, sk_o, vi_s, intra_own, intra_other, dt_sent, share, share_got, total,
+    in_sem, out_sem, par_ss, par_rs, mid_ss, mid_rs, pair_ss, pair_rs, f1_ss, f1_rs, b1_ss, b1_rs, f2_ss, f2_rs, b2_ss, b2_rs,
     back_ss, back_rs, share_ss, share_rs, total_ss, total_rs,
 ):
     me = lax.axis_index("ctx")
@@ -178,8 +179,11 @@
     ends_own[...] = jnp.exp(last)
     here = pl.ds(pl.multiple_of(core * heads_here, heads_here), heads_here)
     pack_pair.wait()
-    _, step_o, cum_o, last_o = steps_of(pack_other[2 * TOKENS :, :], rate_s[here, :], bias_s[here, :])
-    tail_o[...] = jnp.exp(last_o - cum_o) * step_o
+    z_s[...] = z
+    z_other, step_other, cum_o, last_o = steps_of(pack_other[2 * TOKENS :, :], rate_s[here, :], bias_s[here, :])
+    z_o[...] = z_other
+    step_o[...] = step_other
+    tail_o[...] = jnp.exp(last_o - cum_o) * step_other
     grow_o[...] = jnp.exp(cum_o)
     ends_other[...] = jnp.exp(last_o)
     b_other = pack_other[0:TOKENS, :].astype(BF16)
@@ -196,7 +200,7 @@
         for k, (src, dst) in enumerate(
             (
                 (y_out, y_hbm), (dc_out, dc_hbm), (dt_out, dt_hbm), (dx_out, dx_hbm), (db_out, db_hbm),
-                (total, total_got.at[me]),
+                (total, total_got.at[chip]),
             )
         )
     ]
@@ -323,7 +327,10 @@
                 y_t[out, :] = inner
                 d_t[out, :] = back
         dgram_t[...] = acc
-        sk_s[heads, :] = folded(xt8.astype(F32) * gt8.astype(F32), GROUP)
+        x8, g8 = xt8.astype(F32), gt8.astype(F32)
+        sk_s[heads, :] = folded(x8 * g8, GROUP)
+        u_s[heads, :] = folded(g8 * y_t[rows, :], GROUP)
+        vi_s[heads, :] = folded(x8 * d_t[rows, :], GROUP)
         return 0
 
     def turn_of(src, gains, hi_out, lo_out):
@@ -369,6 +376,18 @@
     out_pieces(pre_b, in_b.at[spot], b2_ss, b2_rs)
 
     lax.fori_loop(SPLIT[2], GROUPS, within, 0)
+
+    far = pl.ds(pl.multiple_of((1 - core) * heads_here, heads_here), heads_here)
+    intra_own[0:heads_here, :] = u_s[far, :]
+    intra_own[heads_here:, :] = vi_s[far, :]
+    intra_pair = to(intra_own, intra_other, mid_ss.at[0], mid_rs.at[0], there)
+    intra_pair.start()
+    turn_of(gt, grow_s, egn_hi, egn_lo)
+    turn_of(xt, tail_s, txn_hi, txn_lo)
+    g_hi, g_lo = split(dgram_t[...])
+    db_out[...] = mul(g_hi, c_ref[...]) + mul(g_lo, c_ref[...])
+    t_hi, t_lo = split(jnp.transpose(dgram_t[...]))
+    dc_out[...] = mul(t_hi, b_ref[...]) + mul(t_lo, b_ref[...])
 
     back_f_pair = to(back_f, carried.at[mine], back_ss.at[0], back_rs.at[0], there)
     back_b_pair = to(back_b, later.at[mine], back_ss.at[1], back_rs.at[1], there)
@@ -380,31 +399,31 @@
         carried[piece_rows(r), :] = jnp.where(first, chips, e_other * chips + state_other[at, :])
         back_f[at, :] = jnp.where(first, e_own * chips + state[piece_rows(r), :], chips)
     back_f_pair.start()
-    turn_of(gt, grow_s, egn_hi, egn_lo)
-    back_f_pair.wait()
-
-    dc_out[...] = jnp.zeros_like(dc_out)
-    db_out[...] = jnp.zeros_like(db_out)
-
-    def after_f(g, _):
+    def read(rows, heads):
+        a_hi, a_lo = split(carried[rows, :])
+        return spread(grow_s[heads, :]) * (mul_nt(a_hi, c_ref[...]) + mul_nt(a_lo, c_ref[...]))
+
+    def own_f(k, _):
+        g = core * half_groups + k
         rows, heads = rows_of(g), heads_of(g)
-        a_hi, a_lo = split(carried[rows, :])
-        readout = mul_nt(a_hi, c_ref[...]) + mul_nt(a_lo, c_ref[...])
-        x8, g8 = xt[rows, :].astype(F32), gt[rows, :].astype(F32)
-        y0 = y_t[rows, :] + spread(grow_s[heads, :]) * readout
-        u_s[heads, :] = folded(g8 * y0, GROUP)
-        y_out[:, rows] = jnp.transpose(y0 + spread(skip_s[heads, :]) * x8).astype(BF16)
-        dc_out[...] += mul(egn_hi[:, rows], a_hi) + mul(egn_hi[:, rows], a_lo) + mul(egn_lo[:, rows], a_hi)
+        part = read(rows, heads)
+        y_t[rows, :] += part
+        u_s[heads, :] += folded(gt[rows, :].astype(F32) * part, GROUP)
         return 0
 
-    lax.fori_loop(0, GROUPS, after_f, 0)
-    turn_of(xt, tail_s, txn_hi, txn_lo)
-    g_hi, g_lo = split(dgram_t[...])
-    db_out[...] += mul(g_hi, c_ref[...]) + mul(g_lo, c_ref[...])
-    t_hi, t_lo = split(jnp.transpose(dgram_t[...]))
-    dc_out[...] += mul(t_hi, b_ref[...]) + mul(t_lo, b_ref[...])
-    outs[0].start()
-    outs[1].start()
+    lax.fori_loop(0, half_groups, own_f, 0)
+    intra_pair.wait()
+
+    def other_f(g, _):
+        rows, heads = rows_of(g), heads_of(g)
+        a_hi, a_lo = split(back_f[rows, :])
+        readout = mul_nt(a_hi, c_other) + mul_nt(a_lo, c_other)
+        g8 = g_other[rows, :]
+        u_o[heads, :] = intra_other[heads, :] + grow_o[heads, :] * folded(g8 * readout, GROUP)
+        sk_o[heads, :] = folded(x_other[rows, :] * g8, GROUP)
+        return 0
+
+    lax.fori_loop(0, half_groups, other_f, 0)
 
     to(in_b.at[most], in_b.at[most], b2_ss.at[0], b2_rs.at[0], there).wait_recv()
     for r in range(CHIPS):
@@ -415,70 +434,134 @@
         back_b[at, :] = jnp.where(first, chips, e_own * chips + grad[piece_rows(r), :])
     back_b_pair.start()
 
-    def after_b(g, _):
+    lanes8 = lax.broadcasted_iota(jnp.int32, (GROUP, 128), 1)
+
+    def at_end(value):
+        value = jnp.broadcast_to(jnp.sum(value, axis=1, keepdims=True), (GROUP, 128))
+        return jnp.where(lanes8 == 127, value, 0.0)
+
+    def from_later(l, gains, entries):
+        l_hi, l_lo = split(l)
+        return spread(gains) * (mul_nt(l_hi, entries) + mul_nt(l_lo, entries))
+
+    def after_b(k, _):
+        g = core * half_groups + k
         rows, heads = rows_of(g), heads_of(g)
         l = later[rows, :]
-        l_hi, l_lo = split(l)
-        tq = spread(tail_s[heads, :]) * (mul_nt(l_hi, b_ref[...]) + mul_nt(l_lo, b_ref[...]))
-        x8 = xt[rows, :].astype(F32)
-        d0 = d_t[rows, :] + tq
-        d_t[rows, :] = d0
-        v_s[heads, :] = folded(x8 * d0, GROUP)
-        extra = folded(x8 * tq, GROUP) + ends_own[heads, :] * folded(carried[rows, :] * l, GROUP)
-        extra = jnp.broadcast_to(jnp.sum(extra, axis=1, keepdims=True), (GROUP, 128))
-        lanes = lax.broadcasted_iota(jnp.int32, (GROUP, 128), 1)
-        u_s[heads, :] += jnp.where(lanes == 127, extra, 0.0)
+        tq = from_later(l, tail_s[heads, :], b_ref[...])
+        d_t[rows, :] += tq
+        from_tail = folded(xt[rows, :].astype(F32) * tq, GROUP)
+        v_s[heads, :] = vi_s[heads, :] + from_tail
+        u_s[heads, :] += at_end(from_tail + ends_own[heads, :] * folded(carried[rows, :] * l, GROUP))
+        rows, heads = rows_of(k), heads_of(k)
+        l = back_b[rows, :]
+        from_tail = folded(x_other[rows, :] * from_later(l, tail_o[heads, :], b_other), GROUP)
+        v_o[heads, :] = intra_other[pl.ds(pl.multiple_of(heads_here + k * GROUP, GROUP), GROUP), :] + from_tail
+        u_o[heads, :] += at_end(from_tail + ends_other[heads, :] * folded(back_f[rows, :] * l, GROUP))
         return 0
 
-    lax.fori_loop(core * half_groups, (core + 1) * half_groups, after_b, 0)
-    back_b_pair.wait()
-    lax.fori_loop((1 - core) * half_groups, (2 - core) * half_groups, after_b, 0)
-
-    u, v = u_s[...], v_s[...]
-    step = step_s[...]
-    rate_gain = jnp.exp(rate)
+    lax.fori_loop(0, half_groups, after_b, 0)
+
+    def pair_of(own, other):
+        return jnp.concatenate([own[here, :], other[...]], axis=0)
+
+    u, v, step, zs = pair_of(u_s, u_o), pair_of(v_s, v_o), pair_of(step_s, step_o), pair_of(z_s, z_o)
+    rate_gain = jnp.exp(pair_of(rate_s, rate_s.at[here]))
     dlog = lane_sums(u - v, True)
     dstep = v / step - rate_gain * dlog
-    draw = dstep / (1.0 + jnp.exp(-z))
-    dt_out[...] = draw
-    outs[2].start()
+    draw = dstep / (1.0 + jnp.exp(-zs))
     rate_sum = jnp.sum(dlog * (-rate_gain * step), axis=1, keepdims=True)
     bias_sum = jnp.sum(draw, axis=1, keepdims=True)
-    skip_sum = jnp.sum(sk_s[...], axis=1, keepdims=True)
+    skip_sum = jnp.sum(pair_of(sk_s, sk_o), axis=1, keepdims=True)
     lanes = lax.broadcasted_iota(jnp.int32, square, 1)
-    share[...] = jnp.where(lanes == 0, rate_sum, jnp.where(lanes == 1, bias_sum, jnp.where(lanes == 2, skip_sum, 0.0)))
-
-    def eight(d):
-        return pl.ds(pl.multiple_of(d * 8, 8), 8)
-
-    share_got[dp] = share[eight(dp), :]
-    to_all(lambda k: share.at[eight(lax.rem(dp + k, n_dp))], share_got.at[dp], share_ss, share_rs, "dp", n_dp, dp)
+    sums = jnp.where(lanes == 0, rate_sum, jnp.where(lanes == 1, bias_sum, jnp.where(lanes == 2, skip_sum, 0.0)))
+    share[...] = sums[0:heads_here, :] + sums[heads_here:, :]
+
+    owners = n_dp // 2
+    owner = dp // owners == core
+    for k in range(owners):
+        plane = core * owners + k
+
+        @pl.when(plane != dp)
+        def _():
+            to(share.at[k * 8 : k * 8 + 8], share_got.at[dp], share_ss.at[0], share_rs.at[0], {"dp": plane}).start()
+
+        @pl.when(plane == dp)
+        def _():
+            share_got[dp] = share[k * 8 : k * 8 + 8, :]
+
+    dt_out[here, :] = draw[0:heads_here, :]
+    dt_sent[...] = draw[heads_here:, :]
+    dt_pair = to(dt_sent, dt_out.at[here], mid_ss.at[1], mid_rs.at[1], there)
+    dt_pair.start()
 
     def finish(g, _):
         rows, heads = rows_of(g), heads_of(g)
-        g8 = gt[rows, :].astype(F32)
-        dx_out[:, rows] = jnp.transpose(d_t[rows, :] + spread(skip_s[heads, :]) * g8).astype(BF16)
+        gains = spread(skip_s[heads, :])
+        y_out[:, rows] = jnp.transpose(y_t[rows, :] + gains * xt[rows, :].astype(F32)).astype(BF16)
+        dx_out[:, rows] = jnp.transpose(d_t[rows, :] + gains * gt[rows, :].astype(F32)).astype(BF16)
+        a_hi, a_lo = split(carried[rows, :])
         l_hi, l_lo = split(later[rows, :])
+        dc_out[...] += mul(egn_hi[:, rows], a_hi) + mul(egn_hi[:, rows], a_lo) + mul(egn_lo[:, rows], a_hi)
         db_out[...] += mul(txn_hi[:, rows], l_hi) + mul(txn_hi[:, rows], l_lo) + mul(txn_lo[:, rows], l_hi)
         return 0
 
-    lax.fori_loop(0, GROUPS, finish, 0)
-    outs[3].start()
-    outs[4].start()
-
-    to(share_got.at[seven], share_got.at[seven], share_ss.at[0], share_rs.at[0], {"dp": dp}).wait()
-    summed = share_got[0]
-    for k in range(1, n_dp):
-        summed = summed + share_got[k]
-    total[...] = summed
-    outs[5].start()
-    to_all(lambda k: total, total_got.at[me], total_ss, total_rs, "ctx", n_ctx, me)
+    def finish_far(k, _):
+        g = (1 - core) * half_groups + k
+        rows, heads = rows_of(g), heads_of(g)
+        y_t[rows, :] += read(rows, heads)
+        d_t[rows, :] += from_later(later[rows, :], tail_s[heads, :], b_ref[...])
+        return finish(g, 0)
+
+    def total_sums():
+        @pl.when(owner)
+        def _():
+            to(share_got.at[seven], share_got.at[seven], share_ss.at[0], share_rs.at[0], {"dp": dp}).wait_recv()
+            summed = share_got[0]
+            for k in range(1, n_dp):
+                summed = summed + share_got[k]
+            total[...] = summed
+            outs[5].start()
+            to_all(lambda k: total, total_got.at[chip], total_ss, total_rs, "ctx", n_ctx, me)
+
+    lax.fori_loop(core * half_groups, (core + 1) * half_groups, finish, 0)
+    back_f_pair.wait()
+    back_b_pair.wait()
+    lax.fori_loop(0, FAR, finish_far, 0)
+    total_sums()
+    lax.fori_loop(FAR, half_groups, finish_far, 0)
+    for k in (0, 1, 3, 4):
+        outs[k].start()
+    dt_pair.wait()
+    outs[2].start()
+    b1_all.wait_send()
     all_pieces(pre_b, b2_ss, b2_rs).wait_send()
-    b1_all.wait_send()
-    for copy in outs:
+    for copy in outs[:5]:
         copy.wait()
-    last31 = pl.ds(0, n_ctx - 1)
-    to(total_got.at[last31], total_got.at[last31], total_ss.at[0], total_rs.at[0], {"ctx": me}).wait()
+
+    def tiles(ref, count):
+        return ref.at[pl.ds(0, count)]
+
+    def shares_sent(count):
+        part = share.at[0 : count * 8]
+        to(part, part, share_ss.at[0], share_rs.at[0], there).wait_send()
+
+    def totals_got(count):
+        part = tiles(total_got, count)
+        to(part, part, total_ss.at[0], total_rs.at[0], there).wait_recv()
+
+    @pl.when(owner)
+    def _():
+        shares_sent(owners - 1)
+        outs[5].wait()
+        part = state.at[0 : (n_ctx - 1) * 8]
+        to(part, part, total_ss.at[0], total_rs.at[0], there).wait_send()
+        totals_got(CHIPS - 1)
+
+    @pl.when(jnp.logical_not(owner))
+    def _():
+        shares_sent(owners)
+        totals_got(CHIPS)
 
 
 def write(*refs):
@@ -506,7 +589,7 @@
 
 
 def local(x, b, c, raw, rate, bias, skip, g):
-    n_dp, n_ctx = lax.axis_size("dp"), lax.axis_size("ctx")
+    n_dp = lax.axis_size("dp")
     vmem = pl.BlockSpec(memory_space=pltpu.VMEM)
     hbm = pl.BlockSpec(memory_space=pltpu.HBM)
     wide = (ROWS, 128)
@@ -525,7 +608,7 @@
 
     landing = [
         buf((TOKENS, ROWS), BF16), buf((TOKENS, ROWS), BF16), buf((TOKENS, ENTRIES)), buf((TOKENS, ENTRIES)), buf(small),
-        buf((n_ctx, 8, 128)),
+        buf((CHIPS, 8, 128)),
     ]
     scratch = [
         *landing[:5],
@@ -538,9 +621,9 @@
         buf(small), buf(few), buf(wide), buf(wide), buf(half), buf(half),
         buf(longer), buf(piece), buf(longer), buf(piece),
         buf(piece), buf(piece), buf(half), buf(half), buf(half), buf(half), buf(wide), buf(wide),
-        buf(wide), buf(wide), buf((TOKENS, TOKENS)), buf(small), buf(small), buf(small),
-        buf(small), buf((n_dp, 8, 128)), buf((8, 128)),
-        sems(8), sems(6), sems(1), sems(1), sems(3), sems(3), *[sems(1)] * 8, sems(2), sems(2), *[sems(1)] * 4,
+        buf(wide), buf(wide), buf((TOKENS, TOKENS)), *[buf(small)] * 4, *[buf(few)] * 5, *[buf(small)] * 3, buf(few),
+        buf(few), buf((n_dp, 8, 128)), buf((8, 128)),
+        sems(8), sems(6), sems(1), sems(1), sems(2), sems(2), sems(3), sems(3), *[sems(1)] * 8, sems(2), sems(2), *[sems(1)] * 4,
     ]
     wide_out = jax.ShapeDtypeStruct((TOKENS, ROWS), BF16)
     square_out = jax.ShapeDtypeStruct((TOKENS, ENTRIES), F32)
@@ -548,7 +631,7 @@
     shapes = [wide_out, wide_out, square_out, square_out, dt_shape]
     results = pl.pallas_call(
         layer,
-        out_shape=[*shapes, jax.ShapeDtypeStruct((n_ctx, 8, 128), F32)],
+        out_shape=[*shapes, jax.ShapeDtypeStruct((CHIPS, 8, 128), F32)],
         in_specs=[hbm] * 8,
         out_specs=[hbm] * 6,
         scratch_shapes=scratch,

time: 63 us -> 60.2 us (0.956)
  Pallas kernels: 62.2 us -> 59.4 us
    pallas_call x1, Pallas kernels: 60 us -> 57.2 us  [local(): pl.pallas_call(layer, out_shape=[*shapes, jax.ShapeDtypeStruct((CHIPS, 8,...]
where the time goes in v4:
time: 60.2 us; the launch traced here: 60.1 us
  Pallas kernels  59.4 us (99%)
  between operations  0.64 us (1%)
    pallas_call x1, Pallas kernels, local(): pl.pallas_call(layer, out_shape=[*shapes, jax.ShapeDtypeStruct((CHIPS, 8,...  57.2 us
    pallas_call x1, Pallas kernels, local(): pl.pallas_call(write, out_shape=[*shapes, *[jax.ShapeDtypeStruct((1, 8),...  2.21 us

profile of v4, /device:TPU:1, one launch (start us, length us, event | category | flops | bytes accessed | tf_op | source)
XLA Modules:
  0.0 60.1 jit_solution(15420317755255760365)
XLA Ops:
  0.6 57.2 %layer.1 = (bf16[128,2048]{1,0:T(8,128)(2,1)}, bf16[128,2048]{1,0:T(8,128)(2,1)}, f32[128,128]{1,0:T(8,128)}, f32[128,128]{1,0:T(8,128)}, f32[64,128]{1,0:T(8,128)}, /*index=5*/f32[16,8,128]{2,1,0:T(8,128)}) custom-call(bf16[128,2048]{1,0:T(8,128)(2,1)} %bitcast.13, bf16[128,128]{1,0:T(8,128)(2,1)} %bitcast.15, bf16[128,128]{1,0:T(8,128)(2,1)} %bitcast.16, ...), custom_call_target="tpu_custom_call" | custom-call | tf_op jit(solution)/shard_map/layer/pallas_call | solution.py:632
  57.9 2.2 %write.1 = (bf16[128,2048]{1,0:T(8,128)(2,1)}, bf16[128,2048]{1,0:T(8,128)(2,1)}, f32[128,128]{1,0:T(8,128)}, f32[128,128]{1,0:T(8,128)}, f32[64,128]{1,0:T(8,12...) custom-call(bf16[128,2048]{1,0:T(8,128)(2,1)} %get-tuple-element.22.refs_0_, ...), custom_call_target="tpu_custom_call" | custom-call | tf_op jit(solution)/shard_map/write/pallas_call | solution.py:641

commit v5 on v4

--- a/solution.py
+++ b/solution.py
@@ -56,8 +56,12 @@
         value = value + moved
         shift *= 2
     return value
-SPLIT = (1, 3, 5)
+SPLIT = (0, 3, 5)
 FAR = 1
+
+
+def far_first(size):
+    return sorted(range(1, size), key=lambda k: -min(k, size - k))
 
 
 def layer(
@@ -85,12 +89,6 @@
     def to(src, dst, ss, rs, where):
         return pltpu.make_async_remote_copy(src, dst, ss, rs, device_id=where, device_id_type=MESH)
 
-    barrier = pltpu.get_barrier_semaphore()
-    for k in range(1, n_dp):
-        pl.semaphore_signal(barrier, 1, device_id={"dp": lax.rem(dp + k, n_dp)}, device_id_type=MESH)
-    for k in range(1, n_ctx):
-        pl.semaphore_signal(barrier, 1, device_id={"ctx": lax.rem(me + k, n_ctx)}, device_id_type=MESH)
-
     loads = [
         pltpu.make_async_copy(src, dst, in_sem.at[k])
         for k, (src, dst) in enumerate(
@@ -102,6 +100,11 @@
     ]
     for copy in loads:
         copy.start()
+    barrier = pltpu.get_barrier_semaphore()
+    for k in far_first(n_dp):
+        pl.semaphore_signal(barrier, 1, device_id={"dp": lax.rem(dp + k, n_dp)}, device_id_type=MESH)
+    for k in far_first(n_ctx):
+        pl.semaphore_signal(barrier, 1, device_id={"ctx": lax.rem(me + k, n_ctx)}, device_id_type=MESH)
     for copy in loads[:3]:
         copy.wait()
 
@@ -117,7 +120,7 @@
     pl.semaphore_wait(barrier, n_dp + n_ctx - 2)
 
     def to_all(src, dst, ss, rs, axis, size, index):
-        for k in range(1, size):
+        for k in far_first(size):
             to(src(k), dst, ss.at[0], rs.at[0], {axis: lax.rem(index + k, size)}).start()
 
     to_all(lambda k: par_recv.at[dp], par_recv.at[dp], par_ss, par_rs, "dp", n_dp, dp)
@@ -152,7 +155,8 @@
     gram_t[...] = mul_nt(b_ref[...], c_ref[...])
 
     seven = pl.ds(0, n_dp - 1)
-    to(par_recv.at[seven], par_recv.at[seven], par_ss.at[0], par_rs.at[0], {"dp": dp}).wait()
+    par_all = to(par_recv.at[seven], par_recv.at[seven], par_ss.at[0], par_rs.at[0], {"dp": dp})
+    par_all.wait_recv()
 
     params = par_recv[0]
     for k in range(1, n_dp):
@@ -218,19 +222,17 @@
     def piece_rows(r):
         return pl.ds(pl.multiple_of(core * HALF + r * PIECE, PIECE), PIECE)
 
-    def chip_of(k):
-        return lax.rem(chip + k, CHIPS)
-
-    def chip_id(k):
-        return {"ctx": chip_of(k) * 2 + core}
+    steps_away = [(dx, dy) for dx in range(4) for dy in range(4) if dx or dy]
+    steps_away.sort(key=lambda step: -min(step[0], 4 - step[0]) - min(step[1], 4 - step[1]))
+    far_chips = [lax.rem(chip // 4 + dx, 4) * 4 + lax.rem(chip + dy, 4) for dx, dy in steps_away]
 
     spot = pl.ds(pl.multiple_of(chip * PIECE, PIECE), PIECE)
     others = pl.ds(0, CHIPS - 1)
     most = pl.ds(0, HALF - PIECE)
 
     def out_pieces(src, dst, ss, rs):
-        for k in range(1, CHIPS):
-            to(src.at[chip_of(k)], dst, ss.at[0], rs.at[0], chip_id(k)).start()
+        for target in far_chips:
+            to(src.at[target], dst, ss.at[0], rs.at[0], {"ctx": target * 2 + core}).start()
 
     def all_pieces(src, ss, rs):
         return to(src.at[others], src.at[others], ss.at[0], rs.at[0], there)
@@ -373,7 +375,8 @@
         run = decay_of(q) * run + got_b[q]
     in_b[spot, :] = pre_b[chip]
     all_pieces(pre_f, f2_ss, f2_rs).wait_send()
-    out_pieces(pre_b, in_b.at[spot], b2_ss, b2_rs)
+    for target in far_chips:
+        to(pre_b.at[target], in_b.at[spot], b2_ss.at[0], b2_rs.at[row], {"ctx": target * 2 + core}).start()
 
     lax.fori_loop(SPLIT[2], GROUPS, within, 0)
 
@@ -425,15 +428,6 @@
 
     lax.fori_loop(0, half_groups, other_f, 0)
 
-    to(in_b.at[most], in_b.at[most], b2_ss.at[0], b2_rs.at[0], there).wait_recv()
-    for r in range(CHIPS):
-        at = slice(r * PIECE, (r + 1) * PIECE)
-        e_own, e_other = two(ends_own, r), two(ends_other, r)
-        chips = in_b[at, :]
-        later[piece_rows(r), :] = jnp.where(first, e_other * chips + grad_other[at, :], chips)
-        back_b[at, :] = jnp.where(first, chips, e_own * chips + grad[piece_rows(r), :])
-    back_b_pair.start()
-
     lanes8 = lax.broadcasted_iota(jnp.int32, (GROUP, 128), 1)
 
     def at_end(value):
@@ -444,23 +438,35 @@
         l_hi, l_lo = split(l)
         return spread(gains) * (mul_nt(l_hi, entries) + mul_nt(l_lo, entries))
 
-    def after_b(k, _):
+    def after_b(k, pieces):
+        k = lax.rem(row + 3 - k, 4)
+        part = in_b.at[pl.ds(0, pieces * PIECE)]
+        to(part, part, b2_ss.at[0], b2_rs.at[k], there).wait_recv()
         g = core * half_groups + k
         rows, heads = rows_of(g), heads_of(g)
+        near, few = rows_of(k), heads_of(k)
+        chips = in_b[near, :]
+        later[rows, :] = jnp.where(first, spread(ends_other[few, :]) * chips + grad_other[near, :], chips)
+        back_b[near, :] = jnp.where(first, chips, spread(ends_own[heads, :]) * chips + grad[rows, :])
         l = later[rows, :]
         tq = from_later(l, tail_s[heads, :], b_ref[...])
         d_t[rows, :] += tq
         from_tail = folded(xt[rows, :].astype(F32) * tq, GROUP)
         v_s[heads, :] = vi_s[heads, :] + from_tail
         u_s[heads, :] += at_end(from_tail + ends_own[heads, :] * folded(carried[rows, :] * l, GROUP))
-        rows, heads = rows_of(k), heads_of(k)
+        rows, heads = near, few
         l = back_b[rows, :]
         from_tail = folded(x_other[rows, :] * from_later(l, tail_o[heads, :], b_other), GROUP)
         v_o[heads, :] = intra_other[pl.ds(pl.multiple_of(heads_here + k * GROUP, GROUP), GROUP), :] + from_tail
         u_o[heads, :] += at_end(from_tail + ends_other[heads, :] * folded(back_f[rows, :] * l, GROUP))
+
+    def early_b(k, _):
+        after_b(k, 4)
         return 0
 
-    lax.fori_loop(0, half_groups, after_b, 0)
+    lax.fori_loop(0, half_groups - 1, early_b, 0)
+    after_b(half_groups - 1, 3)
+    back_b_pair.start()
 
     def pair_of(own, other):
         return jnp.concatenate([own[here, :], other[...]], axis=0)
@@ -521,8 +527,8 @@
             for k in range(1, n_dp):
                 summed = summed + share_got[k]
             total[...] = summed
+            to_all(lambda k: total, total_got.at[chip], total_ss, total_rs, "ctx", n_ctx, me)
             outs[5].start()
-            to_all(lambda k: total, total_got.at[chip], total_ss, total_rs, "ctx", n_ctx, me)
 
     lax.fori_loop(core * half_groups, (core + 1) * half_groups, finish, 0)
     back_f_pair.wait()
@@ -534,6 +540,7 @@
         outs[k].start()
     dt_pair.wait()
     outs[2].start()
+    par_all.wait_send()
     b1_all.wait_send()
     all_pieces(pre_b, b2_ss, b2_rs).wait_send()
     for copy in outs[:5]:
@@ -623,7 +630,7 @@
         buf(piece), buf(piece), buf(half), buf(half), buf(half), buf(half), buf(wide), buf(wide),
         buf(wide), buf(wide), buf((TOKENS, TOKENS)), *[buf(small)] * 4, *[buf(few)] * 5, *[buf(small)] * 3, buf(few),
         buf(few), buf((n_dp, 8, 128)), buf((8, 128)),
-        sems(8), sems(6), sems(1), sems(1), sems(2), sems(2), sems(3), sems(3), *[sems(1)] * 8, sems(2), sems(2), *[sems(1)] * 4,
+        sems(8), sems(6), sems(1), sems(1), sems(2), sems(2), sems(3), sems(3), *[sems(1)] * 7, sems(4), sems(2), sems(2), *[sems(1)] * 4,
     ]
     wide_out = jax.ShapeDtypeStruct((TOKENS, ROWS), BF16)
     square_out = jax.ShapeDtypeStruct((TOKENS, ENTRIES), F32)

time: 60.2 us -> 59.4 us (0.987)
  Pallas kernels: 59.4 us -> 58.6 us
    pallas_call x1, Pallas kernels: 57.2 us -> 56.4 us  [local(): pl.pallas_call(layer, out_shape=[*shapes, jax.ShapeDtypeStruct((CHIPS, 8,...]
where the time goes in v5:
time: 59.4 us; the launch traced here: 59.2 us
  Pallas kernels  58.6 us (99%)
  between operations  0.64 us (1%)
    pallas_call x1, Pallas kernels, local(): pl.pallas_call(layer, out_shape=[*shapes, jax.ShapeDtypeStruct((CHIPS, 8,...  56.4 us
    pallas_call x1, Pallas kernels, local(): pl.pallas_call(write, out_shape=[*shapes, *[jax.ShapeDtypeStruct((1, 8),...  2.21 us

profile of v5, /device:TPU:1, one launch (start us, length us, event | category | flops | bytes accessed | tf_op | source)
XLA Modules:
  0.0 59.2 jit_solution(6761151959045223217)
XLA Ops:
  0.6 56.4 %layer.1 = (bf16[128,2048]{1,0:T(8,128)(2,1)}, bf16[128,2048]{1,0:T(8,128)(2,1)}, f32[128,128]{1,0:T(8,128)}, f32[128,128]{1,0:T(8,128)}, f32[64,128]{1,0:T(8,128)}, /*index=5*/f32[16,8,128]{2,1,0:T(8,128)}) custom-call(bf16[128,2048]{1,0:T(8,128)(2,1)} %bitcast.13, bf16[128,128]{1,0:T(8,128)(2,1)} %bitcast.15, bf16[128,128]{1,0:T(8,128)(2,1)} %bitcast.16, ...), custom_call_target="tpu_custom_call" | custom-call | tf_op jit(solution)/shard_map/layer/pallas_call | solution.py:639
  57.0 2.2 %write.1 = (bf16[128,2048]{1,0:T(8,128)(2,1)}, bf16[128,2048]{1,0:T(8,128)(2,1)}, f32[128,128]{1,0:T(8,128)}, f32[128,128]{1,0:T(8,128)}, f32[64,128]{1,0:T(8,12...) custom-call(bf16[128,2048]{1,0:T(8,128)(2,1)} %get-tuple-element.22.refs_0_, ...), custom_call_target="tpu_custom_call" | custom-call | tf_op jit(solution)/shard_map/write/pallas_call | solution.py:648

commit v6 on v5

--- a/solution.py
+++ b/solution.py
@@ -430,6 +430,15 @@
 
     lanes8 = lax.broadcasted_iota(jnp.int32, (GROUP, 128), 1)
 
+    def pair_of(own, other):
+        return jnp.concatenate([own[here, :], other[...]], axis=0)
+
+    rate_gain = jnp.exp(pair_of(rate_s, rate_s.at[here]))
+    slope = 1.0 / (1.0 + jnp.exp(-pair_of(z_s, z_o)))
+    weight = slope / pair_of(step_s, step_o)
+    reach = rate_gain * lane_sums(slope, False)
+    cum_both = jnp.concatenate([cum_s[here, :], cum_o], axis=0)
+
     def at_end(value):
         value = jnp.broadcast_to(jnp.sum(value, axis=1, keepdims=True), (GROUP, 128))
         return jnp.where(lanes8 == 127, value, 0.0)
@@ -468,16 +477,10 @@
     after_b(half_groups - 1, 3)
     back_b_pair.start()
 
-    def pair_of(own, other):
-        return jnp.concatenate([own[here, :], other[...]], axis=0)
-
-    u, v, step, zs = pair_of(u_s, u_o), pair_of(v_s, v_o), pair_of(step_s, step_o), pair_of(z_s, z_o)
-    rate_gain = jnp.exp(pair_of(rate_s, rate_s.at[here]))
-    dlog = lane_sums(u - v, True)
-    dstep = v / step - rate_gain * dlog
-    draw = dstep / (1.0 + jnp.exp(-zs))
-    rate_sum = jnp.sum(dlog * (-rate_gain * step), axis=1, keepdims=True)
-    bias_sum = jnp.sum(draw, axis=1, keepdims=True)
+    u, v = pair_of(u_s, u_o), pair_of(v_s, v_o)
+    dcum = u - v
+    rate_sum = jnp.sum(dcum * cum_both, axis=1, keepdims=True)
+    bias_sum = jnp.sum(v * weight - dcum * reach, axis=1, keepdims=True)
     skip_sum = jnp.sum(pair_of(sk_s, sk_o), axis=1, keepdims=True)
     lanes = lax.broadcasted_iota(jnp.int32, square, 1)
     sums = jnp.where(lanes == 0, rate_sum, jnp.where(lanes == 1, bias_sum, jnp.where(lanes == 2, skip_sum, 0.0)))
@@ -496,6 +499,7 @@
         def _():
             share_got[dp] = share[k * 8 : k * 8 + 8, :]
 
+    draw = weight * v - slope * rate_gain * lane_sums(dcum, True)
     dt_out[here, :] = draw[0:heads_here, :]
     dt_sent[...] = draw[heads_here:, :]
     dt_pair = to(dt_sent, dt_out.at[here], mid_ss.at[1], mid_rs.at[1], there)

time: 59.4 us -> 58.9 us (level)
  no operation moved by 1% of the time
where the time goes in v6:
time: 58.9 us; the launch traced here: 58.8 us
  Pallas kernels  58.1 us (99%)
  between operations  0.64 us (1%)
    pallas_call x1, Pallas kernels, local(): pl.pallas_call(layer, out_shape=[*shapes, jax.ShapeDtypeStruct((CHIPS, 8,...  55.9 us
    pallas_call x1, Pallas kernels, local(): pl.pallas_call(write, out_shape=[*shapes, *[jax.ShapeDtypeStruct((1, 8),...  2.21 us

profile of v6, /device:TPU:1, one launch (start us, length us, event | category | flops | bytes accessed | tf_op | source)
XLA Modules:
  0.0 58.8 jit_solution(9821020423302196230)
XLA Ops:
  0.6 55.9 %layer.1 = (bf16[128,2048]{1,0:T(8,128)(2,1)}, bf16[128,2048]{1,0:T(8,128)(2,1)}, f32[128,128]{1,0:T(8,128)}, f32[128,128]{1,0:T(8,128)}, f32[64,128]{1,0:T(8,128)}, /*index=5*/f32[16,8,128]{2,1,0:T(8,128)}) custom-call(bf16[128,2048]{1,0:T(8,128)(2,1)} %bitcast.13, bf16[128,128]{1,0:T(8,128)(2,1)} %bitcast.15, bf16[128,128]{1,0:T(8,128)(2,1)} %bitcast.16, ...), custom_call_target="tpu_custom_call" | custom-call | tf_op jit(solution)/shard_map/layer/pallas_call | solution.py:643
  56.6 2.2 %write.1 = (bf16[128,2048]{1,0:T(8,128)(2,1)}, bf16[128,2048]{1,0:T(8,128)(2,1)}, f32[128,128]{1,0:T(8,128)}, f32[128,128]{1,0:T(8,128)}, f32[64,128]{1,0:T(8,12...) custom-call(bf16[128,2048]{1,0:T(8,128)(2,1)} %get-tuple-element.22.refs_0_, ...), custom_call_target="tpu_custom_call" | custom-call | tf_op jit(solution)/shard_map/write/pallas_call | solution.py:652
